TPU v7x, 32 devices: a whole 2x2x4 slice. The times are simulated.
32 devices in a mesh: img: 4 (over y, x), cls: 8 (over z, core).
Axes of the slice: x: 2, y: 2, z: 4, core: 2. Of those that a mesh axis runs over, the one named last changes fastest.
Arguments:
- images: bfloat16 [3072, 256, 256], P(('img', 'cls')), may hold values from -6 to 6
- ctf_table: float32 [16, 128, 256], replicated, may hold values from -1 to 1
- defocus_bin: int32 [3072], P(('img', 'cls')), may hold values from 0 to 15
- projections: bfloat16 [8, 8, 128, 256], P('cls'), may hold values from -6 to 6
- best_class: int32 [3072, 1], P(('img', 'cls')), may hold values from 0 to 7; in each aligned block of 96 rows (0 to 95, 96 to 191, ...) at most 36 rows name the same one
- best_orient: int32 [3072], P(('img', 'cls')), may hold values from 0 to 7
- slice_slots: int32 [8, 128], replicated, may hold values from 0 to 511
- slot_weight: float32 [8, 128], replicated, may hold values from 0.25 to 1
Outputs:
- best_score: float32 [3072], P(('img', 'cls'))
- data_volume: float32 [8, 512, 256], P('cls', 'img')
- weight_volume: float32 [8, 512, 256], P('cls', 'img')
Inputs may be any that keep to these rules, and one draw needn't show every extreme that they name: `best_class`: among the 96 images of one device (aligned blocks of rows), at most 36 name the same class, a bound that some blocks reach.
All inputs are finite; a program needn't handle non-finite values.
Results may differ from a plain program's by a relative error of at most 0.0052.
Values may be sent and summed in bfloat16 or wider, within the bound.
No kernel may reach another device: no remote copies, remote signals or barrier semaphores. Data moves between devices by JAX's collectives and lax.ppermute only.
A program may use at most 192 MiB of HBM per device.

v0:
```python
import functools
import math

import jax
import jax.numpy as jnp
import numpy as np
from jax import lax
from jax.experimental import pallas as pl
from jax.experimental.pallas import tpu as pltpu
from jax.sharding import PartitionSpec as P

SLOTS = 512
BLOCK = 16


def dft_tables(pixels):
    half = pixels // 2
    position = np.arange(pixels)
    norm = 1.0 / math.sqrt(pixels)
    angle_cols = (position[:, None] * np.arange(half)[None, :] % pixels) * (2.0 * math.pi / pixels)
    col_table = np.concatenate([np.cos(angle_cols), -np.sin(angle_cols)], axis=1) * norm
    angle_rows = ((np.arange(half) - half // 2)[:, None] * position[None, :] % pixels) * (
        2.0 * math.pi / pixels
    )
    row_table = np.concatenate([np.cos(angle_rows), np.sin(angle_rows)], axis=0) * norm
    to_bf = lambda t: jnp.asarray(t.astype(np.float32), jnp.bfloat16)
    return to_bf(col_table), to_bf(row_table)


def front_kernel(
    blocks, pair_ref, bin_ref, core_ref, img_ref, col_ref, row_ref, ctf_ref, slot_ref, wt_ref,
    w2_ref, keep_ref, send_ref, acc, wscr, hot, hi_scr, lo_scr,
):
    step = pl.program_id(0)
    half = col_ref.shape[0] // 2
    orients = wt_ref.shape[1]
    rows = wt_ref.shape[0]
    number = img_ref.shape[0]

    @pl.when(step == 0)
    def _():
        acc[...] = jnp.zeros_like(acc)
        slots = lax.broadcasted_iota(jnp.int32, hot.shape, 0)
        hot[...] = jnp.where(slots == slot_ref[...], 1.0, 0.0).astype(jnp.bfloat16)

    @pl.when(step < blocks)
    def _():
        for i in range(number):
            one = jnp.dot(img_ref[i], col_ref[...], preferred_element_type=jnp.float32)
            both = jnp.dot(
                row_ref[...], one.astype(jnp.bfloat16), preferred_element_type=jnp.float32
            )
            index = step * number + i
            which_bin, which_pair = bin_ref[index], pair_ref[index]
            real = both[:rows, :half] + both[rows:, half:]
            imag = both[:rows, half:] - both[rows:, :half]
            for part, spec in enumerate((real, imag)):
                lanes = pl.ds(part * half, half)
                weighted = (spec * ctf_ref[which_bin, :, lanes]).astype(jnp.bfloat16)
                weighted = weighted.astype(jnp.float32)
                acc[which_pair, :, lanes] += weighted
                wscr[part, pl.ds(i * rows, rows), :] = weighted
        for j in range(rows):
            w2_ref[j] = jnp.concatenate(
                [
                    wscr[part, pl.ds(j, number, stride=rows), :]
                    for part in range(2)
                ],
                axis=1,
            ).astype(jnp.bfloat16)

    @pl.when(step >= blocks)
    def _():
        z = step - blocks
        core = core_ref[0]
        for part, which in enumerate((2 * z + core, 2 * z + 1 - core)):
            for o in range(orients):
                value = acc[which * orients + o] * wt_ref[:, o : o + 1]
                high = value.astype(jnp.bfloat16)
                low = (value - high.astype(jnp.float32)).astype(jnp.bfloat16)
                where = (pl.ds(o * rows, rows), pl.ds(part * 2 * half, 2 * half))
                hi_scr[where] = high
                lo_scr[where] = low
        slab = jnp.dot(hot[...], hi_scr[...], preferred_element_type=jnp.float32) + jnp.dot(
            hot[...], lo_scr[...], preferred_element_type=jnp.float32
        )
        keep_ref[0] = slab[:, : 2 * half]
        send_ref[0] = slab[:, 2 * half :].astype(jnp.bfloat16)


def front(images, ctf_table, pair, bins, core, slots_row, weight_cols, classes):
    number, pixels = images.shape[0], images.shape[1]
    bin_count, rows = ctf_table.shape[0], ctf_table.shape[1]
    orients = weight_cols.shape[1]
    col_table, row_table = dft_tables(pixels)
    blocks, groups = number // BLOCK, classes // 2
    at_block = lambda i: jnp.minimum(i, blocks - 1)
    at_group = lambda i: jnp.maximum(i - blocks, 0)
    whole = lambda shape: pl.BlockSpec(
        shape, lambda i, *_: (0,) * len(shape), pipeline_mode=pl.Buffered(1)
    )
    return pl.pallas_call(
        functools.partial(front_kernel, blocks),
        grid_spec=pltpu.PrefetchScalarGridSpec(
            num_scalar_prefetch=3,
            grid=(blocks + groups,),
            in_specs=[
                pl.BlockSpec((BLOCK, pixels, pixels), lambda i, *_: (at_block(i), 0, 0)),
                whole((pixels, pixels)),
                whole((pixels, pixels)),
                whole((bin_count, rows, pixels)),
                whole((1, orients * rows)),
                whole((rows, orients)),
            ],
            out_specs=[
                pl.BlockSpec((rows, BLOCK, pixels), lambda i, *_: (0, at_block(i), 0)),
                pl.BlockSpec((1, SLOTS, pixels), lambda i, *_: (at_group(i), 0, 0)),
                pl.BlockSpec((1, SLOTS, pixels), lambda i, *_: (at_group(i), 0, 0)),
            ],
            scratch_shapes=[
                pltpu.VMEM((classes * orients, rows, pixels), jnp.float32),
                pltpu.VMEM((2, BLOCK * rows, pixels // 2), jnp.float32),
                pltpu.VMEM((SLOTS, orients * rows), jnp.bfloat16),
                pltpu.VMEM((orients * rows, 2 * pixels), jnp.bfloat16),
                pltpu.VMEM((orients * rows, 2 * pixels), jnp.bfloat16),
            ],
        ),
        out_shape=[
            jax.ShapeDtypeStruct((rows, number, pixels), jnp.bfloat16),
            jax.ShapeDtypeStruct((groups, SLOTS, pixels), jnp.float32),
            jax.ShapeDtypeStruct((groups, SLOTS, pixels), jnp.bfloat16),
        ],
        compiler_params=pltpu.CompilerParams(vmem_limit_bytes=50 * 2**20),
        name="front",
    )(pair, bins, core, images, col_table, row_table, ctf_table, slots_row, weight_cols)


def score_kernel(w_ref, p_ref, best_ref, acc):
    step = pl.program_id(0)

    @pl.when(step == 0)
    def _():
        acc[...] = jnp.zeros_like(acc)

    total = acc[...]
    classes, depth, orients, pixels = p_ref.shape
    for j in range(depth):
        panel = jnp.concatenate([p_ref[c, j] for c in range(classes)], axis=0)
        total = total + lax.dot_general(
            panel, w_ref[j], (((1,), (1,)), ((), ())), preferred_element_type=jnp.float32
        )
    acc[...] = total

    @pl.when(step == pl.num_programs(0) - 1)
    def _():
        scale = 1.0 / math.sqrt(pl.num_programs(0) * depth * pixels)
        best_ref[...] = jnp.max(total * scale, axis=0, keepdims=True)


def score(w2, panel, depth=16):
    rows, number, pixels = w2.shape
    classes, orients = panel.shape[0], panel.shape[2]
    return pl.pallas_call(
        score_kernel,
        grid=(rows // depth,),
        in_specs=[
            pl.BlockSpec((depth, number, pixels), lambda i: (i, 0, 0)),
            pl.BlockSpec((classes, depth, orients, pixels), lambda i: (0, i, 0, 0)),
        ],
        out_specs=pl.BlockSpec((1, number), lambda i: (0, 0)),
        scratch_shapes=[pltpu.VMEM((classes * orients, number), jnp.float32)],
        out_shape=jax.ShapeDtypeStruct((1, number), jnp.float32),
        compiler_params=pltpu.CompilerParams(vmem_limit_bytes=32 * 2**20),
        name="score",
    )(w2, panel)


def power_kernel(tally_ref, ctf_ref, slot_ref, wt_ref, start_ref, out_ref, squares, scr):
    bin_count, rows, pixels = ctf_ref.shape
    orients = wt_ref.shape[1]
    for b in range(bin_count):
        squares[b] = ctf_ref[b] * ctf_ref[b]
    for o in range(orients):
        value = squares[0] * tally_ref[o * bin_count]
        for b in range(1, bin_count):
            value = value + squares[b] * tally_ref[o * bin_count + b]
        value = value * wt_ref[:, o : o + 1]
        for part in range(3):
            piece = value.astype(jnp.bfloat16)
            scr[pl.ds(o * rows, rows), pl.ds(part * pixels, pixels)] = piece
            value = value - piece.astype(jnp.float32)
    target = lax.broadcasted_iota(jnp.int32, (out_ref.shape[0], orients * rows), 0) + start_ref[0]
    hot = jnp.where(target == slot_ref[...], 1.0, 0.0).astype(jnp.bfloat16)
    slab = jnp.dot(hot, scr[...], preferred_element_type=jnp.float32)
    out_ref[...] = (
        slab[:, 2 * pixels :] + slab[:, pixels : 2 * pixels]
    ) + slab[:, :pixels]


def power_slab(own_tally, ctf_table, slots_row, weight_cols, start, slab_rows):
    bin_count, rows, pixels = ctf_table.shape
    orients = weight_cols.shape[1]
    vmem = pl.BlockSpec(memory_space=pltpu.VMEM)
    smem = pl.BlockSpec(memory_space=pltpu.SMEM)
    return pl.pallas_call(
        power_kernel,
        in_specs=[smem, vmem, vmem, vmem, smem],
        out_specs=vmem,
        out_shape=jax.ShapeDtypeStruct((slab_rows, pixels), jnp.float32),
        scratch_shapes=[
            pltpu.VMEM((bin_count, rows, pixels), jnp.float32),
            pltpu.VMEM((orients * rows, 3 * pixels), jnp.bfloat16),
        ],
        compiler_params=pltpu.CompilerParams(vmem_limit_bytes=16 * 2**20),
        name="power",
    )(own_tally, ctf_table, slots_row, weight_cols, start)


def swap(value, axis, mask):
    size = lax.axis_size(axis)
    return lax.ppermute(value, axis, [(i, i ^ mask) for i in range(size)])


def on_device(
    images, ctf_table, defocus_bin, projections, best_class, best_orient, slice_slots, slot_weight
):
    orients = projections.shape[1]
    bin_count = ctf_table.shape[0]
    classes, imgs = lax.axis_size("cls"), lax.axis_size("img")
    my_cls, my_img = lax.axis_index("cls"), lax.axis_index("img")
    core, my_z = my_cls % 2, my_cls // 2
    groups, slab_rows = classes // 2, SLOTS // imgs
    pixels = images.shape[1]

    panel = lax.all_gather(jnp.transpose(projections, (0, 2, 1, 3)), "cls", axis=0, tiled=True)

    class_ids = best_class[:, 0]
    pair = class_ids * orients + best_orient
    tally_key = pair * bin_count + defocus_bin
    tally_hot = tally_key[:, None] == jnp.arange(classes * orients * bin_count, dtype=jnp.int32)
    tallies = lax.psum(jnp.sum(tally_hot.astype(jnp.float32), axis=0), ("img", "cls"))
    own_tally = lax.dynamic_slice_in_dim(
        tallies, my_cls * (orients * bin_count), orients * bin_count
    )

    slots_row = slice_slots.reshape(1, -1)
    weight_cols = slot_weight.T
    w2, keep, send = front(
        images, ctf_table, pair, defocus_bin, core[None], slots_row, weight_cols, classes
    )
    best = score(w2, panel)
    weight_slab = power_slab(
        own_tally, ctf_table, slots_row, weight_cols, (my_img * slab_rows)[None], slab_rows
    )

    chip = keep + swap(send, "cls", 1).astype(jnp.float32)
    chip = chip.reshape(groups, imgs, slab_rows, pixels)
    part = lambda mask: lax.dynamic_index_in_dim(chip, my_img ^ mask, 1, keepdims=False)
    own = part(0)
    for got in [swap(part(m).astype(jnp.bfloat16), "img", m) for m in range(1, imgs)]:
        own = own + got.astype(jnp.float32)
    part_z = lambda mask: lax.dynamic_index_in_dim(own, my_z ^ mask, 0, keepdims=False)
    data = part_z(0)
    for got in [swap(part_z(m).astype(jnp.bfloat16), "cls", 2 * m) for m in range(1, groups)]:
        data = data + got.astype(jnp.float32)
    return (best.reshape(-1), data[None], weight_slab[None])


def solution(mesh):
    return jax.shard_map(
        on_device,
        mesh=mesh,
        in_specs=(
            P(("img", "cls"), None, None),
            P(),
            P(("img", "cls")),
            P("cls", None, None, None),
            P(("img", "cls"), None),
            P(("img", "cls")),
            P(),
            P(),
        ),
        out_specs=(P(("img", "cls")), P("cls", "img", None), P("cls", "img", None)),
        check_vma=False,
    )
```

profile of v0, /device:TPU:0, one launch (start us, length us, event | category | flops | bytes accessed | tf_op | source)
XLA Modules:
  0.0 129.4 jit_solution(13010989234323032343)
XLA Ops:
  7.2 0.0 all-gather.2.cloned.1.call-start
  7.2 2.2 %copy.32 = bf16[1,8,128,256]{3,1,2,0:T(8,128)(2,1)} copy(bf16[1,8,128,256]{3,2,1,0:T(8,128)(2,1)} %param.13) | data formatting | bytes 1048576 | tf_op args[3]
  9.4 0.0 all-gather.2.cloned.1.call-update
  9.4 0.8 copy.23
  10.2 0.7 multiply_add_fusion
  10.9 0.9 copy-done.3
  11.8 0.9 copy-done.4
  12.7 0.7 copy-done.5
  13.4 0.7 copy-done.7
  14.1 28.6 %front.1 = (bf16[128,96,256]{2,1,0:T(8,128)(2,1)}, f32[4,512,256]{2,1,0:T(8,128)S(1)}, bf16[4,512,256]{2,1,0:T(8,128)(2,1)S(1)}) custom-call(s32[96]{0:T(128)S(1)} %get-tuple-element.10.pair_ref, s32[96]{0:T(128)S(1)} %copy-done.7, s32[1]{0:T(128)} %bitcast.1.core_ref, bf16[96,256,256]{2,1,0:T(8,128)(2,1)} %img_ref.1, bf16[256,256]{1,0:T(8,128)(2,1)S(1)} %copy-done.3, ...), custom_call_target="tpu_custom_call" | custom-call | tf_op jit(solution)/shard_map/front/pallas_call | solution.py:102
  42.7 0.5 collective-permute-start
  43.1 2.4 %collective-permute-done = bf16[4,512,256]{2,1,0:T(8,128)(2,1)} collective-permute-done((bf16[4,512,256]{2,1,0:T(8,128)(2,1)S(1)}, bf16[4,512,256]{2,1,0:T(8,128)(2,1)}, u32[]{:S(2)}, u32[]{:S(2)}) %collective-permute-start) | collective-permute-done | bytes 1048608 | tf_op jit(solution)/shard_map/ppermute | solution.py:221
  45.5 1.5 %convert_add_fusion = f32[4,512,256]{2,1,0:T(8,128)S(1)} fusion(f32[4,512,256]{2,1,0:T(8,128)S(1)} %get-tuple-element.7, bf16[4,512,256]{2,1,0:T(8,128)(2,1)} %collective-permute-done), kind=kLoop, calls=%fused_computation | loop fusion | flops 1048576 | bytes 5242880 | tf_op jit(solution)/shard_map/add | solution.py:256
  47.1 1.3 %copy-done.8 = f32[4,512,256]{2,1,0:T(8,128)} copy-done((f32[4,512,256]{2,1,0:T(8,128)}, f32[4,512,256]{2,1,0:T(8,128)S(1)}, u32[]{:S(2)}) %copy-start.8) | copy-done | bytes 2097176
  48.3 0.1 fusion.2
  48.4 2.9 %collective-permute-start.1 = (bf16[4,128,256]{2,1,0:T(8,128)(2,1)S(1)}, bf16[4,128,256]{2,1,0:T(8,128)(2,1)S(1)}, u32[]{:S(2)}, u32[]{:S(2)}) collective-permute-start(bf16[4,128,256]{2,1,0:T(8,128)(2,1)S(1)} %get-tuple-element.11), channel_id=1, source_target_pairs={{0,8},{8,0},{16,24},{24,16},{1,9},{9,1},{17,25},{25,17},{2,10},{10... | collective-permute-start | bytes 786440 | tf_op jit(solution)/shard_map/ppermute | solution.py:221
  51.4 1.5 %collective-permute-start.2 = (bf16[4,128,256]{2,1,0:T(8,128)(2,1)S(1)}, bf16[4,128,256]{2,1,0:T(8,128)(2,1)S(1)}, u32[]{:S(2)}, u32[]{:S(2)}) collective-permute-start(bf16[4,128,256]{2,1,0:T(8,128)(2,1)S(1)} %get-tuple-element.12), channel_id=1, source_target_pairs={{0,16},{8,24},{16,0},{24,8},{1,17},{9,25},{17,1},{25,9},{2,18},{10... | collective-permute-start | bytes 786440 | tf_op jit(solution)/shard_map/ppermute | solution.py:221
  52.9 0.0 collective-permute-start.3
  52.9 5.6 %collective-permute-done.1 = bf16[4,128,256]{2,1,0:T(8,128)(2,1)S(1)} collective-permute-done((bf16[4,128,256]{2,1,0:T(8,128)(2,1)S(1)}, bf16[4,128,256]{2,1,0:T(8,128)(2,1)S(1)}, u32[]{:S(2)}, u32[]{:S(2)}) %collective-permute-start.1) | collective-permute-done | bytes 262176 | tf_op jit(solution)/shard_map/ppermute | solution.py:221
  58.5 6.6 %collective-permute-done.2 = bf16[4,128,256]{2,1,0:T(8,128)(2,1)S(1)} collective-permute-done((bf16[4,128,256]{2,1,0:T(8,128)(2,1)S(1)}, bf16[4,128,256]{2,1,0:T(8,128)(2,1)S(1)}, u32[]{:S(2)}, u32[]{:S(2)}) %collective-permute-start.2) | collective-permute-done | bytes 262176 | tf_op jit(solution)/shard_map/ppermute | solution.py:221
  65.1 1.3 fusion.1
  66.4 1.6 %collective-permute-start.4 = (bf16[128,256]{1,0:T(8,128)(2,1)S(1)}, bf16[128,256]{1,0:T(8,128)(2,1)S(1)}, u32[]{:S(2)}, u32[]{:S(2)}) collective-permute-start(bf16[128,256]{1,0:T(8,128)(2,1)S(1)} %get-tuple-element.14), channel_id=1, source_target_pairs={{0,2},{1,3},{2,0},{3,1},{4,6},{5,7},{6,4},{7,5},{8,10},{9,11},{10,... | collective-permute-start | bytes 196616 | tf_op jit(solution)/shard_map/ppermute | solution.py:221
  68.0 2.6 %collective-permute-start.5 = (bf16[128,256]{1,0:T(8,128)(2,1)S(1)}, bf16[128,256]{1,0:T(8,128)(2,1)S(1)}, u32[]{:S(2)}, u32[]{:S(2)}) collective-permute-start(bf16[128,256]{1,0:T(8,128)(2,1)S(1)} %get-tuple-element.16), channel_id=1, source_target_pairs={{0,4},{1,5},{2,6},{3,7},{4,0},{5,1},{6,2},{7,3},{8,12},{9,13},{10,... | collective-permute-start | bytes 196616 | tf_op jit(solution)/shard_map/ppermute | solution.py:221
  70.6 0.2 collective-permute-start.6
  70.8 0.1 convert_reduce_fusion
  70.9 39.0 %psum.7 = f32[1024]{0:T(1024)S(1)} all-reduce(f32[1024]{0:T(1024)S(1)} %convert_reduce_fusion), channel_id=1, replica_groups=mesh['img'=4,'cls'=8] {'img','cls'}, use_global_device_ids=true, to_apply=%region_1.2 | all-reduce | flops 1024 | bytes 8192 | tf_op jit(solution)/shard_map/psum | solution.py:241
  109.9 0.1 dynamic_slice.37.tally_ref
  110.0 2.9 %power.1 = f32[128,256]{1,0:T(8,128)} custom-call(f32[128]{0:T(128)S(1)} %dynamic_slice.37.tally_ref, f32[16,128,256]{2,1,0:T(8,128)S(1)} %copy-done, s32[1,1024]{1,0:T(1,128)S(1)} %bitcast.56, f32[128,8]{1,0:T(8,128)S(1)} %bitcast.54, s32[1]{0:T(128)} %bitcast.16.start_ref), custom_call_target="tpu_custom_call" | custom-call | tf_op jit(solution)/shard_map/power/pallas_call | solution.py:205
  112.9 0.7 fusion.7
  113.6 2.8 %copy-done.1 = bf16[128,96,256]{2,1,0:T(8,128)(2,1)S(1)} copy-done((bf16[128,96,256]{2,1,0:T(8,128)(2,1)S(1)}, bf16[128,96,256]{2,1,0:T(8,128)(2,1)}, u32[]{:S(2)}) %copy-start.1) | copy-done | bytes 6291480
  116.4 2.2 %copy-done.2 = bf16[8,128,8,256]{3,2,1,0:T(8,128)(2,1)S(1)} copy-done((bf16[8,128,8,256]{3,2,1,0:T(8,128)(2,1)S(1)}, bf16[8,128,8,256]{3,2,1,0:T(8,128)(2,1)}, u32[]{:S(2)}) %copy-start.2) | copy-done | bytes 4194328
  118.5 4.0 %score.1 = f32[1,96]{1,0:T(1,128)} custom-call(bf16[128,96,256]{2,1,0:T(8,128)(2,1)S(1)} %copy-done.1, bf16[8,128,8,256]{3,2,1,0:T(8,128)(2,1)S(1)} %copy-done.2), custom_call_target="tpu_custom_call" | custom-call | tf_op jit(solution)/shard_map/score/pallas_call | solution.py:163
  (17 shorter events, 0.1 us)
Async XLA Ops:
  7.2 106.4 %all-gather.2.cloned.1.call-start = ((), (), s32[]{:S(2)}) async-start(), calls=%async_computation | async-start | bytes 4718592 | tf_op jit(solution)/shard_map/all_gather | solution.py:235
  10.9 0.9 copy-start.3
  11.8 0.9 copy-start.4
  12.7 0.7 copy-start.5
  13.4 0.7 copy-start.7
  42.7 2.9 %collective-permute-start = (bf16[4,512,256]{2,1,0:T(8,128)(2,1)S(1)}, bf16[4,512,256]{2,1,0:T(8,128)(2,1)}, u32[]{:S(2)}, u32[]{:S(2)}) collective-permute-start(bf16[4,512,256]{2,1,0:T(8,128)(2,1)S(1)} %get-tuple-element.8), channel_id=1, source_target_pairs={{0,1},{1,0},{2,3},{3,2},{4,5},{5,4},{6,7},{7,6},{8,9},{9,8},{10,11... | collective-permute-start | bytes 3145736 | tf_op jit(solution)/shard_map/ppermute | solution.py:221
  47.0 1.3 %copy-start.8 = (f32[4,512,256]{2,1,0:T(8,128)}, f32[4,512,256]{2,1,0:T(8,128)S(1)}, u32[]{:S(2)}) copy-start(f32[4,512,256]{2,1,0:T(8,128)S(1)} %convert_add_fusion) | copy-start | bytes 6291460
  47.0 63.0 %copy-start = (f32[16,128,256]{2,1,0:T(8,128)S(1)}, f32[16,128,256]{2,1,0:T(8,128)}, u32[]{:S(2)}) copy-start(f32[16,128,256]{2,1,0:T(8,128)} %ctf_ref.3) | copy-start | bytes 6291460
  47.0 63.0 %copy-start.6 = (s32[8,128]{1,0:T(8,128)S(1)}, s32[8,128]{1,0:T(8,128)}, u32[]{:S(2)}) copy-start(s32[8,128]{1,0:T(8,128)} %param.16) | copy-start | bytes 12292
  48.4 10.0 %collective-permute-start.1 = (bf16[4,128,256]{2,1,0:T(8,128)(2,1)S(1)}, bf16[4,128,256]{2,1,0:T(8,128)(2,1)S(1)}, u32[]{:S(2)}, u32[]{:S(2)}) collective-permute-start(bf16[4,128,256]{2,1,0:T(8,128)(2,1)S(1)} %get-tuple-element.11), channel_id=1, source_target_pairs={{0,8},{8,0},{16,24},{24,16},{1,9},{9,1},{17,25},{25,17},{2,10},{10... | collective-permute-start | bytes 786440 | tf_op jit(solution)/shard_map/ppermute | solution.py:221
  51.4 13.7 %collective-permute-start.2 = (bf16[4,128,256]{2,1,0:T(8,128)(2,1)S(1)}, bf16[4,128,256]{2,1,0:T(8,128)(2,1)S(1)}, u32[]{:S(2)}, u32[]{:S(2)}) collective-permute-start(bf16[4,128,256]{2,1,0:T(8,128)(2,1)S(1)} %get-tuple-element.12), channel_id=1, source_target_pairs={{0,16},{8,24},{16,0},{24,8},{1,17},{9,25},{17,1},{25,9},{2,18},{10... | collective-permute-start | bytes 786440 | tf_op jit(solution)/shard_map/ppermute | solution.py:221
  52.9 12.2 %collective-permute-start.3 = (bf16[4,128,256]{2,1,0:T(8,128)(2,1)S(1)}, bf16[4,128,256]{2,1,0:T(8,128)(2,1)}, u32[]{:S(2)}, u32[]{:S(2)}) collective-permute-start(bf16[4,128,256]{2,1,0:T(8,128)(2,1)S(1)} %get-tuple-element.13), channel_id=1, source_target_pairs={{0,24},{8,16},{16,8},{24,0},{1,25},{9,17},{17,9},{25,1},{2,26},{10... | collective-permute-start | bytes 786440 | tf_op jit(solution)/shard_map/ppermute | solution.py:221
  66.4 46.5 %collective-permute-start.4 = (bf16[128,256]{1,0:T(8,128)(2,1)S(1)}, bf16[128,256]{1,0:T(8,128)(2,1)S(1)}, u32[]{:S(2)}, u32[]{:S(2)}) collective-permute-start(bf16[128,256]{1,0:T(8,128)(2,1)S(1)} %get-tuple-element.14), channel_id=1, source_target_pairs={{0,2},{1,3},{2,0},{3,1},{4,6},{5,7},{6,4},{7,5},{8,10},{9,11},{10,... | collective-permute-start | bytes 196616 | tf_op jit(solution)/shard_map/ppermute | solution.py:221
  68.0 44.9 %collective-permute-start.5 = (bf16[128,256]{1,0:T(8,128)(2,1)S(1)}, bf16[128,256]{1,0:T(8,128)(2,1)S(1)}, u32[]{:S(2)}, u32[]{:S(2)}) collective-permute-start(bf16[128,256]{1,0:T(8,128)(2,1)S(1)} %get-tuple-element.16), channel_id=1, source_target_pairs={{0,4},{1,5},{2,6},{3,7},{4,0},{5,1},{6,2},{7,3},{8,12},{9,13},{10,... | collective-permute-start | bytes 196616 | tf_op jit(solution)/shard_map/ppermute | solution.py:221
  70.6 42.3 %collective-permute-start.6 = (bf16[128,256]{1,0:T(8,128)(2,1)S(1)}, bf16[128,256]{1,0:T(8,128)(2,1)S(1)}, u32[]{:S(2)}, u32[]{:S(2)}) collective-permute-start(bf16[128,256]{1,0:T(8,128)(2,1)S(1)} %get-tuple-element.15), channel_id=1, source_target_pairs={{0,6},{1,7},{2,4},{3,5},{4,2},{5,3},{6,0},{7,1},{8,14},{9,15},{10,... | collective-permute-start | bytes 196616 | tf_op jit(solution)/shard_map/ppermute | solution.py:221
  113.6 2.8 %copy-start.1 = (bf16[128,96,256]{2,1,0:T(8,128)(2,1)S(1)}, bf16[128,96,256]{2,1,0:T(8,128)(2,1)}, u32[]{:S(2)}) copy-start(bf16[128,96,256]{2,1,0:T(8,128)(2,1)} %get-tuple-element.6.w_ref) | copy-start | bytes 18874372
  116.4 2.2 %copy-start.2 = (bf16[8,128,8,256]{3,2,1,0:T(8,128)(2,1)S(1)}, bf16[8,128,8,256]{3,2,1,0:T(8,128)(2,1)}, u32[]{:S(2)}) copy-start(bf16[8,128,8,256]{3,2,1,0:T(8,128)(2,1)} %all-gather.2.cloned.1.call-done.p_ref) | copy-start | bytes 12582916
Sparse Core Ops, SparseCore 0:
  9.6 49.8 all-gather.1
where the time goes:
time: 130 us; the launch traced here: 129 us
  blocking collectives  39 us (30%)
  Pallas kernels  35.5 us (27%)
  waiting for transfers between devices  14.6 us (11%)
  between operations  14.1 us (11%)
  local copies, waits for them, and re-layouts  12.6 us (10%)
  starting transfers between devices  9.4 us (7%)
  other arithmetic  4.21 us (3%)
    psum x1, blocking collectives, on_device(): lax.psum(jnp.sum(tally_hot.astype(jnp.float32), axis=0), ('img', 'cls'))  39 us
    pallas_call x1, Pallas kernels, front(): pl.pallas_call(functools.partial(front_kernel, blocks), grid_spec=pltpu.P...  28.6 us
    ppermute x7, waiting for transfers between devices, swap(): return lax.ppermute(value, axis, [(i, i ^ mask) for i in range(size)])  14.6 us
    unnamed x20, local copies, waits for them, and re-layouts  12.4 us
    ppermute x7, starting transfers between devices, swap(): return lax.ppermute(value, axis, [(i, i ^ mask) for i in range(size)])  9.37 us
    pallas_call x1, Pallas kernels, score(): pl.pallas_call(score_kernel, grid=(rows // depth,), in_specs=[pl.BlockSpe...  4.03 us
    pallas_call x1, Pallas kernels, power_slab(): pl.pallas_call(power_kernel, in_specs=[smem, vmem, vmem, vmem, smem], out...  2.86 us
  transfers between devices with their start and end apart: 8, of which 3 were waited for; matrix products, arithmetic and copies ran while one was open for 4% of the time, Pallas kernels for 24%

commit v1 on v0

v1 whole, which is shorter than its diff:
```python
import functools
import math

import jax
import jax.numpy as jnp
import numpy as np
from jax import lax
from jax.experimental import pallas as pl
from jax.experimental.pallas import tpu as pltpu
from jax.sharding import PartitionSpec as P

SLOTS = 512
BLOCK = 16


def dft_tables(pixels):
    half = pixels // 2
    position = np.arange(pixels)
    norm = 1.0 / math.sqrt(pixels)
    angle_cols = (position[:, None] * np.arange(half)[None, :] % pixels) * (2.0 * math.pi / pixels)
    col_table = np.concatenate([np.cos(angle_cols), -np.sin(angle_cols)], axis=1) * norm
    angle_rows = ((np.arange(half) - half // 2)[:, None] * position[None, :] % pixels) * (
        2.0 * math.pi / pixels
    )
    row_table = np.concatenate([np.cos(angle_rows), np.sin(angle_rows)], axis=0) * norm
    return jnp.asarray(np.stack([col_table, row_table]).astype(np.float32), jnp.bfloat16)


def front_kernel(
    blocks, class_ref, orient_ref, bin_ref, img_ref, table_ref, ctf_ref, slot_ref, wt_ref, w2_ref,
    keep_ref, send_ref, count_ref, acc, wscr, hot, value_scr, counts, wt_scr,
):
    step = pl.program_id(0)
    half = table_ref.shape[1] // 2
    orients, rows = wt_ref.shape
    number = img_ref.shape[0]

    @pl.when(step == 0)
    def _():
        acc[...] = jnp.zeros_like(acc)
        counts[...] = jnp.zeros_like(counts)
        wt_scr[...] = jnp.transpose(wt_ref[...])
        slots = lax.broadcasted_iota(jnp.int32, (hot.shape[0], rows), 0)
        for o in range(orients):
            hot[:, pl.ds(o * rows, rows)] = jnp.where(
                slots == slot_ref[o : o + 1, :], 1.0, 0.0
            ).astype(jnp.bfloat16)

    @pl.when(step < blocks)
    def _():
        lane = lax.broadcasted_iota(jnp.int32, (1, counts.shape[2]), 1)
        for i in range(number):
            one = jnp.dot(img_ref[i], table_ref[0], preferred_element_type=jnp.float32)
            both = jnp.dot(
                table_ref[1], one.astype(jnp.bfloat16), preferred_element_type=jnp.float32
            )
            index = step * number + i
            which_bin = bin_ref[index]
            which_class, which_orient = class_ref[index], orient_ref[index]
            which_pair = which_class * orients + which_orient
            counted = (which_class, pl.ds(which_orient, 1), slice(None))
            counts[counted] += jnp.where(lane == which_bin, 1.0, 0.0)
            real = both[:rows, :half] + both[rows:, half:]
            imag = both[:rows, half:] - both[rows:, :half]
            for part, spec in enumerate((real, imag)):
                lanes = pl.ds(part * half, half)
                weighted = (spec * ctf_ref[which_bin, :, lanes]).astype(jnp.bfloat16)
                weighted = weighted.astype(jnp.float32)
                acc[which_pair, :, lanes] += weighted
                wscr[part, pl.ds(i * (rows + 8), rows), :] = weighted
        for j in range(rows):
            w2_ref[j] = jnp.concatenate(
                [
                    wscr[part, pl.ds(j, number, stride=rows + 8), :]
                    for part in range(2)
                ],
                axis=1,
            ).astype(jnp.bfloat16)

    @pl.when(step >= blocks)
    def _():
        z = step - blocks
        core = lax.axis_index("cls") % 2
        for part, which in enumerate((2 * z + core, 2 * z + 1 - core)):
            for o in range(orients):
                value = acc[which * orients + o] * wt_scr[:, o : o + 1]
                value_scr[pl.ds(o * rows, rows), pl.ds(part * 2 * half, 2 * half)] = value.astype(
                    jnp.bfloat16
                )
        slab = jnp.dot(hot[...], value_scr[...], preferred_element_type=jnp.float32)
        keep_ref[0] = slab[:, : 2 * half]
        send_ref[0, : SLOTS] = slab[:, 2 * half :].astype(jnp.bfloat16)
        send_ref[0, SLOTS :, : half] = counts[2 * z + 1 - core].astype(jnp.bfloat16)
        send_ref[0, SLOTS :, half :] = jnp.zeros((orients, half), jnp.bfloat16)
        count_ref[0] = counts[2 * z + core]


def front(images, ctf_table, class_ids, orient_ids, bins, slice_slots, slot_weight, classes):
    number, pixels = images.shape[0], images.shape[1]
    bin_count, rows = ctf_table.shape[0], ctf_table.shape[1]
    orients = slot_weight.shape[0]
    blocks, groups = number // BLOCK, classes // 2
    at_block = lambda i: jnp.minimum(i, blocks - 1)
    at_group = lambda i: jnp.maximum(i - blocks, 0)
    whole = lambda shape: pl.BlockSpec(
        shape, lambda i, *_: (0,) * len(shape), pipeline_mode=pl.Buffered(1)
    )
    return pl.pallas_call(
        functools.partial(front_kernel, blocks),
        grid_spec=pltpu.PrefetchScalarGridSpec(
            num_scalar_prefetch=3,
            grid=(blocks + groups,),
            in_specs=[
                pl.BlockSpec((BLOCK, pixels, pixels), lambda i, *_: (at_block(i), 0, 0)),
                whole((2, pixels, pixels)),
                whole((bin_count, rows, pixels)),
                whole((orients, rows)),
                whole((orients, rows)),
            ],
            out_specs=[
                pl.BlockSpec((rows, BLOCK, pixels), lambda i, *_: (0, at_block(i), 0)),
                pl.BlockSpec((1, SLOTS, pixels), lambda i, *_: (at_group(i), 0, 0)),
                pl.BlockSpec((1, SLOTS + orients, pixels), lambda i, *_: (at_group(i), 0, 0)),
                pl.BlockSpec((1, orients, pixels // 2), lambda i, *_: (at_group(i), 0, 0)),
            ],
            scratch_shapes=[
                pltpu.VMEM((classes * orients, rows, pixels), jnp.float32),
                pltpu.VMEM((2, BLOCK * (rows + 8), pixels // 2), jnp.float32),
                pltpu.VMEM((SLOTS, orients * rows), jnp.bfloat16),
                pltpu.VMEM((orients * rows, 2 * pixels), jnp.bfloat16),
                pltpu.VMEM((classes, orients, pixels // 2), jnp.float32),
                pltpu.VMEM((rows, orients), jnp.float32),
            ],
        ),
        out_shape=[
            jax.ShapeDtypeStruct((rows, number, pixels), jnp.bfloat16),
            jax.ShapeDtypeStruct((groups, SLOTS, pixels), jnp.float32),
            jax.ShapeDtypeStruct((groups, SLOTS + orients, pixels), jnp.bfloat16),
            jax.ShapeDtypeStruct((groups, orients, pixels // 2), jnp.float32),
        ],
        compiler_params=pltpu.CompilerParams(vmem_limit_bytes=60 * 2**20),
        cost_estimate=pl.CostEstimate(
            flops=8 * number * pixels**3, bytes_accessed=number * pixels**2 * 4, transcendentals=0
        ),
        name="front",
    )(class_ids, orient_ids, bins, images, dft_tables(pixels), ctf_table, slice_slots, slot_weight)


def score_kernel(w_ref, panel_ref, best_ref, acc):
    step = pl.program_id(0)

    @pl.when(step == 0)
    def _():
        acc[...] = jnp.zeros_like(acc)

    total = acc[...]
    for j in range(w_ref.shape[0]):
        panel = [panel_ref[c, j] for c in range(panel_ref.shape[0])]
        total = total + lax.dot_general(
            jnp.concatenate(panel, axis=0),
            w_ref[j],
            (((1,), (1,)), ((), ())),
            preferred_element_type=jnp.float32,
        )
    acc[...] = total

    @pl.when(step == pl.num_programs(0) - 1)
    def _():
        scale = 1.0 / math.sqrt(pl.num_programs(0) * w_ref.shape[0] * w_ref.shape[2])
        best_ref[...] = jnp.max(acc[...] * scale, axis=0, keepdims=True)


def score(w2, panel, depth=16):
    rows, number, pixels = w2.shape
    classes, orients = panel.shape[0], panel.shape[2]
    return pl.pallas_call(
        score_kernel,
        grid=(rows // depth,),
        in_specs=[
            pl.BlockSpec((depth, number, pixels), lambda i: (i, 0, 0)),
            pl.BlockSpec((classes, depth, orients, pixels), lambda i: (0, i, 0, 0)),
        ],
        out_specs=pl.BlockSpec((1, number), lambda i: (0, 0)),
        scratch_shapes=[pltpu.VMEM((classes * orients, number), jnp.float32)],
        out_shape=jax.ShapeDtypeStruct((1, number), jnp.float32),
        compiler_params=pltpu.CompilerParams(vmem_limit_bytes=60 * 2**20),
        name="score",
    )(w2, panel)


def chip_kernel(masks, keep_ref, count_ref, got_ref, own_ref, own_count_ref, *outs):
    size = own_ref.shape[1]
    slots = keep_ref.shape[1]
    lanes = count_ref.shape[2]
    count = count_ref[...] + got_ref[:, pl.ds(slots, 8), pl.ds(0, lanes)].astype(jnp.float32)
    own_count_ref[...] = count

    def part(mask):
        rows = pl.ds(pl.multiple_of((lax.axis_index("img") ^ mask) * size, size), size)
        return keep_ref[:, rows, :] + got_ref[:, rows, :].astype(jnp.float32)

    own_ref[...] = part(0)
    for mask, out_ref in zip(masks, outs, strict=True):
        out_ref[:, pl.ds(0, size), :] = part(mask).astype(jnp.bfloat16)
        tail = count.astype(jnp.bfloat16)
        out_ref[:, pl.ds(size, 8), :] = jnp.concatenate([tail, jnp.zeros_like(tail)], axis=2)


def chip_sum(keep, count, got, imgs):
    groups, slots, pixels = keep.shape
    size = slots // imgs
    masks = tuple(range(1, imgs))
    at = lambda shape: pl.BlockSpec((1, *shape[1:]), lambda i: (i, 0, 0))
    out_shape = [
        jax.ShapeDtypeStruct((groups, size, pixels), jnp.float32),
        jax.ShapeDtypeStruct(count.shape, jnp.float32),
    ] + [jax.ShapeDtypeStruct((groups, size + 8, pixels), jnp.bfloat16)] * (imgs - 1)
    return pl.pallas_call(
        functools.partial(chip_kernel, masks),
        grid=(groups,),
        in_specs=[at(keep.shape), at(count.shape), at(got.shape)],
        out_specs=[at(out.shape) for out in out_shape],
        out_shape=out_shape,
        compiler_params=pltpu.CompilerParams(vmem_limit_bytes=12 * 2**20),
        name="chip_sum",
    )(keep, count, got)


def plane_kernel(masks, own_ref, count_ref, *refs):
    gots, outs = refs[: len(refs) - len(masks) - 2], refs[len(refs) - len(masks) - 2 :]
    data_ref, data_count_ref, sends = outs[0], outs[1], outs[2:]
    size, lanes = own_ref.shape[1], count_ref.shape[2]

    def part(mask):
        z = (lax.axis_index("cls") // 2) ^ mask
        data, count = own_ref[z], count_ref[z]
        for got in gots:
            data = data + got[z, pl.ds(0, size), :].astype(jnp.float32)
            count = count + got[z, pl.ds(size, 8), pl.ds(0, lanes)].astype(jnp.float32)
        return data, count

    data_ref[...], data_count_ref[...] = part(0)
    for mask, send_ref in zip(masks, sends, strict=True):
        data, count = part(mask)
        high = jnp.floor(count * (1.0 / 128.0)) * 128.0
        send_ref[pl.ds(0, size), :] = data.astype(jnp.bfloat16)
        send_ref[pl.ds(size, 8), :] = jnp.concatenate([high, count - high], axis=1).astype(
            jnp.bfloat16
        )


def plane_sum(own, count, gots):
    groups, size, pixels = own.shape
    vmem = pl.BlockSpec()
    masks = tuple(range(1, groups))
    return pl.pallas_call(
        functools.partial(plane_kernel, masks),
        in_specs=[vmem] * (2 + len(gots)),
        out_specs=[vmem] * (groups + 1),
        out_shape=[
            jax.ShapeDtypeStruct((size, pixels), jnp.float32),
            jax.ShapeDtypeStruct(count.shape[1:], jnp.float32),
        ]
        + [jax.ShapeDtypeStruct((size + 8, pixels), jnp.bfloat16)] * (groups - 1),
        compiler_params=pltpu.CompilerParams(vmem_limit_bytes=12 * 2**20),
        name="plane_sum",
    )(own, count, *gots)


def final_kernel(ctf_ref, slot_ref, wt_ref, own_ref, count_ref, *refs):
    gots, (data_ref, weight_ref, squares, scr) = refs[:-4], refs[-4:]
    bin_count, rows, pixels = ctf_ref.shape
    size, orients, lanes = own_ref.shape[0], wt_ref.shape[0], count_ref.shape[1]
    wt_cols = jnp.transpose(wt_ref[...])
    data, count = own_ref[...], count_ref[...]
    for got in gots:
        data = data + got[pl.ds(0, size), :].astype(jnp.float32)
        tail = got[pl.ds(size, 8), :].astype(jnp.float32)
        count = count + (tail[:, :lanes] + tail[:, lanes:])
    data_ref[...] = data
    for b in range(bin_count):
        squares[b] = ctf_ref[b] * ctf_ref[b]
    for o in range(orients):
        value = squares[0] * count[o : o + 1, 0:1]
        for b in range(1, bin_count):
            value = value + squares[b] * count[o : o + 1, b : b + 1]
        value = value * wt_cols[:, o : o + 1]
        for part in range(3):
            piece = value.astype(jnp.bfloat16)
            scr[pl.ds(o * rows, rows), pl.ds(part * pixels, pixels)] = piece
            value = value - piece.astype(jnp.float32)
    target = lax.broadcasted_iota(jnp.int32, (size, rows), 0) + lax.axis_index("img") * size
    hot = jnp.concatenate(
        [
            jnp.where(target == slot_ref[o : o + 1, :], 1.0, 0.0).astype(jnp.bfloat16)
            for o in range(orients)
        ],
        axis=1,
    )
    slab = jnp.dot(hot, scr[...], preferred_element_type=jnp.float32)
    weight_ref[...] = (slab[:, 2 * pixels :] + slab[:, pixels : 2 * pixels]) + slab[:, :pixels]


def final_sum(ctf_table, slice_slots, slot_weight, own, count, gots):
    bin_count, rows, pixels = ctf_table.shape
    orients = slot_weight.shape[0]
    vmem = pl.BlockSpec()
    return pl.pallas_call(
        final_kernel,
        in_specs=[vmem] * (5 + len(gots)),
        out_specs=[vmem, vmem],
        out_shape=[jax.ShapeDtypeStruct(own.shape, jnp.float32)] * 2,
        scratch_shapes=[
            pltpu.VMEM((bin_count, rows, pixels), jnp.float32),
            pltpu.VMEM((orients * rows, 3 * pixels), jnp.bfloat16),
        ],
        compiler_params=pltpu.CompilerParams(vmem_limit_bytes=12 * 2**20),
        name="final_sum",
    )(ctf_table, slice_slots, slot_weight, own, count, *gots)


def swap(value, axis, mask):
    size = lax.axis_size(axis)
    return lax.ppermute(value, axis, [(i, i ^ mask) for i in range(size)])


def on_device(
    images, ctf_table, defocus_bin, projections, best_class, best_orient, slice_slots, slot_weight
):
    classes, imgs = lax.axis_size("cls"), lax.axis_size("img")
    own_panel = jnp.transpose(projections, (0, 2, 1, 3))
    panel = lax.all_gather(own_panel, "cls", axis=0, tiled=True)
    w2, keep, send, count = front(
        images,
        ctf_table,
        best_class.reshape(-1),
        best_orient,
        defocus_bin,
        slice_slots,
        slot_weight,
        classes,
    )
    got = swap(send, "cls", 1)
    own, own_count, *parts = chip_sum(keep, count, got, imgs)
    gots = [swap(part, "img", m + 1) for m, part in enumerate(parts)]
    data, data_count, *parts = plane_sum(own, own_count, gots)
    gots = [swap(part, "cls", 2 * (m + 1)) for m, part in enumerate(parts)]
    best = score(w2, panel)
    gots, best = lax.optimization_barrier((gots, best))
    data, weight = final_sum(ctf_table, slice_slots, slot_weight, data, data_count, gots)
    return (best.reshape(-1), data[None], weight[None])


def solution(mesh):
    return jax.shard_map(
        on_device,
        mesh=mesh,
        in_specs=(
            P(("img", "cls"), None, None),
            P(),
            P(("img", "cls")),
            P("cls", None, None, None),
            P(("img", "cls"), None),
            P(("img", "cls")),
            P(),
            P(),
        ),
        out_specs=(P(("img", "cls")), P("cls", "img", None), P("cls", "img", None)),
        check_vma=False,
    )
```

time: 130 us -> 78.1 us (0.60)
  blocking collectives: 39 us -> 0 us
  local copies, waits for them, and re-layouts: 12.6 us -> 4.5 us
  other arithmetic: 4.21 us -> 0 us
  Pallas kernels: 35.5 us -> 31.3 us
  waiting for transfers between devices: 14.6 us -> 18.2 us
    psum x1 -> x0, blocking collectives: 39 us -> none  [on_device(): lax.psum(jnp.sum(tally_hot.astype(jnp.float32), axis=0), ('img', 'cls'))]
    pallas_call x1, Pallas kernels: 28.6 us -> 20.3 us  [front(): pl.pallas_call(functools.partial(front_kernel, blocks), grid_spec=pltpu.P...]
    unnamed x20 -> x11, local copies, waits for them, and re-layouts: 12.4 us -> 4.5 us
    pallas_call x1, Pallas kernels: 4.03 us -> 8.11 us  [score(): pl.pallas_call(score_kernel, grid=(rows // depth,), in_specs=[pl.BlockSpe...]
    add x3 -> x0, other arithmetic: 3.41 us -> none  [the longest x1 1.46 us: on_device(): chip = keep + swap(send, 'cls', 1).astype(jnp.float32)]
    all_gather x1, waiting for transfers between devices: 0.01 us -> 2.79 us  [on_device(): panel = lax.all_gather(own_panel, 'cls', axis=0, tiled=True)]
    pallas_call x1 -> x3, Pallas kernels: 2.86 us -> 2.97 us  [the longest x1 2.54 us: final_sum(): pl.pallas_call(final_kernel, in_specs=[vmem] * (5 + len(gots)), out_specs...]
  transfers between devices with their start and end apart: 8 -> 8, of which waited for: 3 -> 4; matrix products, arithmetic and copies ran while one was open for 4% -> 0% of each run, Pallas kernels for 24% -> 37%
where the time goes in v1:
time: 78.1 us; the launch traced here: 77.6 us
  Pallas kernels  31.3 us (40%)
  waiting for transfers between devices  18.2 us (23%)
  between operations  14.1 us (18%)
  starting transfers between devices  9.49 us (12%)
  local copies, waits for them, and re-layouts  4.5 us (6%)
    pallas_call x1, Pallas kernels, front(): pl.pallas_call(functools.partial(front_kernel, blocks), grid_spec=pltpu.P...  20.3 us
    ppermute x7, waiting for transfers between devices, swap(): return lax.ppermute(value, axis, [(i, i ^ mask) for i in range(size)])  15.4 us
    ppermute x7, starting transfers between devices, swap(): return lax.ppermute(value, axis, [(i, i ^ mask) for i in range(size)])  9.45 us
    pallas_call x1, Pallas kernels, score(): pl.pallas_call(score_kernel, grid=(rows // depth,), in_specs=[pl.BlockSpe...  8.11 us
    unnamed x11, local copies, waits for them, and re-layouts  4.5 us
    all_gather x1, waiting for transfers between devices, on_device(): panel = lax.all_gather(own_panel, 'cls', axis=0, tiled=True)  2.79 us
    pallas_call x1, Pallas kernels, final_sum(): pl.pallas_call(final_kernel, in_specs=[vmem] * (5 + len(gots)), out_specs...  2.54 us
  transfers between devices with their start and end apart: 8, of which 4 were waited for; matrix products, arithmetic and copies ran while one was open for 0% of the time, Pallas kernels for 37%

profile of v1, /device:TPU:0, one launch (start us, length us, event | category | flops | bytes accessed | tf_op | source)
XLA Modules:
  0.0 77.6 jit_solution(14418835851719483745)
XLA Ops:
  7.2 0.0 all-gather.2.cloned.1.call-start
  7.2 2.1 %copy.15 = bf16[1,8,128,256]{3,1,2,0:T(8,128)(2,1)} copy(bf16[1,8,128,256]{3,2,1,0:T(8,128)(2,1)} %param.12) | data formatting | bytes 1048576 | tf_op args[3]
  9.4 0.0 all-gather.2.cloned.1.call-update
  9.4 20.3 %front.1 = (bf16[128,96,256]{2,1,0:T(8,128)(2,1)}, f32[4,512,256]{2,1,0:T(8,128)}, bf16[4,520,256]{2,1,0:T(8,128)(2,1)}, f32[4,8,128]{2,1,0:T(8,128)}) custom-call(s32[96]{0:T(128)} %bitcast.11, s32[96]{0:T(128)} %orient_ref.1, s32[96]{0:T(128)} %bin_ref.1, bf16[96,256,256]{2,1,0:T(8,128)(2,1)} %img_ref.1, bf16[2,256,256]{2,1,0:T(8,128)(2,1)} %constant.2.clone.table_ref, ...), custom_call_target="tpu_custom_call" | custom-call | flops 12884901888 | bytes 25165824 | tf_op jit(solution)/shard_map/front/pallas_call | solution.py:108
  29.6 0.5 collective-permute-start
  30.2 2.5 %collective-permute-done.got_ref = bf16[4,520,256]{2,1,0:T(8,128)(2,1)S(1)} collective-permute-done((bf16[4,520,256]{2,1,0:T(8,128)(2,1)}, bf16[4,520,256]{2,1,0:T(8,128)(2,1)S(1)}, u32[]{:S(2)}, u32[]{:S(2)}) %collective-permute-start) | collective-permute-done | bytes 1064992 | tf_op jit(solution)/shard_map/ppermute | solution.py:324
  32.7 0.0 copy-start.1
  32.7 1.6 %copy-done.1 = f32[4,512,256]{2,1,0:T(8,128)S(1)} copy-done((f32[4,512,256]{2,1,0:T(8,128)S(1)}, f32[4,512,256]{2,1,0:T(8,128)}, u32[]{:S(2)}) %copy-start.1) | copy-done | bytes 2097176
  34.3 0.0 copy-start.2
  34.3 0.7 copy-done.2
  35.0 0.3 chip_sum.1
  35.3 2.9 %collective-permute-start.1 = (bf16[4,136,256]{2,1,0:T(8,128)(2,1)S(1)}, bf16[4,136,256]{2,1,0:T(8,128)(2,1)S(1)}, u32[]{:S(2)}, u32[]{:S(2)}) collective-permute-start(bf16[4,136,256]{2,1,0:T(8,128)(2,1)S(1)} %get-tuple-element.28), channel_id=1, source_target_pairs={{0,8},{8,0},{16,24},{24,16},{1,9},{9,1},{17,25},{25,17},{2,10},{10... | collective-permute-start | bytes 835592 | tf_op jit(solution)/shard_map/ppermute | solution.py:324
  38.2 1.5 %collective-permute-start.2 = (bf16[4,136,256]{2,1,0:T(8,128)(2,1)S(1)}, bf16[4,136,256]{2,1,0:T(8,128)(2,1)S(1)}, u32[]{:S(2)}, u32[]{:S(2)}) collective-permute-start(bf16[4,136,256]{2,1,0:T(8,128)(2,1)S(1)} %get-tuple-element.29), channel_id=1, source_target_pairs={{0,16},{8,24},{16,0},{24,8},{1,17},{9,25},{17,1},{25,9},{2,18},{10... | collective-permute-start | bytes 835592 | tf_op jit(solution)/shard_map/ppermute | solution.py:324
  39.7 0.0 collective-permute-start.3
  39.8 5.9 %collective-permute-done.1.refs_0_ = bf16[4,136,256]{2,1,0:T(8,128)(2,1)S(1)} collective-permute-done((bf16[4,136,256]{2,1,0:T(8,128)(2,1)S(1)}, bf16[4,136,256]{2,1,0:T(8,128)(2,1)S(1)}, u32[]{:S(2)}, u32[]{:S(2)}) %collective-permute-start.1) | collective-permute-done | bytes 278560 | tf_op jit(solution)/shard_map/ppermute | solution.py:324
  45.7 6.9 %collective-permute-done.2.refs_1_ = bf16[4,136,256]{2,1,0:T(8,128)(2,1)S(1)} collective-permute-done((bf16[4,136,256]{2,1,0:T(8,128)(2,1)S(1)}, bf16[4,136,256]{2,1,0:T(8,128)(2,1)S(1)}, u32[]{:S(2)}, u32[]{:S(2)}) %collective-permute-start.2) | collective-permute-done | bytes 278560 | tf_op jit(solution)/shard_map/ppermute | solution.py:324
  52.6 0.0 collective-permute-done.3.refs_2_
  52.6 0.1 plane_sum.1
  52.7 1.7 %collective-permute-start.4 = (bf16[136,256]{1,0:T(8,128)(2,1)S(1)}, bf16[136,256]{1,0:T(8,128)(2,1)S(1)}, u32[]{:S(2)}, u32[]{:S(2)}) collective-permute-start(bf16[136,256]{1,0:T(8,128)(2,1)S(1)} %get-tuple-element.31), channel_id=1, source_target_pairs={{0,2},{1,3},{2,0},{3,1},{4,6},{5,7},{6,4},{7,5},{8,10},{9,11},{10,... | collective-permute-start | bytes 208904 | tf_op jit(solution)/shard_map/ppermute | solution.py:324
  54.4 2.8 %collective-permute-start.5 = (bf16[136,256]{1,0:T(8,128)(2,1)S(1)}, bf16[136,256]{1,0:T(8,128)(2,1)S(1)}, u32[]{:S(2)}, u32[]{:S(2)}) collective-permute-start(bf16[136,256]{1,0:T(8,128)(2,1)S(1)} %get-tuple-element.32), channel_id=1, source_target_pairs={{0,4},{1,5},{2,6},{3,7},{4,0},{5,1},{6,2},{7,3},{8,12},{9,13},{10,... | collective-permute-start | bytes 208904 | tf_op jit(solution)/shard_map/ppermute | solution.py:324
  57.2 0.0 collective-permute-start.6
  57.2 2.8 %all-gather.2.cloned.1.call-done.panel_ref = bf16[8,128,8,256]{3,2,1,0:T(8,128)(2,1)} async-done(((bf16[1,128,8,256]{3,2,1,0:T(8,128)(2,1)}), bf16[8,128,8,256]{3,2,1,0:T(8,128)(2,1)}) %all-gather.2.cloned.1.call-update) | async-done | bytes 4194320 | tf_op jit(solution)/shard_map/all_gather | solution.py:332
  60.0 0.0 copy-start
  60.0 0.0 copy-start.3
  60.0 8.1 %score.1 = f32[1,96]{1,0:T(1,128)} custom-call(bf16[128,96,256]{2,1,0:T(8,128)(2,1)} %get-tuple-element.34.w_ref, bf16[8,128,8,256]{3,2,1,0:T(8,128)(2,1)} %all-gather.2.cloned.1.call-done.panel_ref), custom_call_target="tpu_custom_call" | custom-call | tf_op jit(solution)/shard_map/score/pallas_call | solution.py:176
  68.1 0.0 collective-permute-done.4.refs_0_
  68.1 0.0 collective-permute-done.5.refs_1_
  68.1 0.0 collective-permute-done.6.refs_2_
  68.2 0.0 copy-done
  68.2 0.0 copy-done.3
  68.2 0.0 copy-done.4
  68.2 2.5 %final_sum.1 = (f32[128,256]{1,0:T(8,128)}, f32[128,256]{1,0:T(8,128)}) custom-call(f32[16,128,256]{2,1,0:T(8,128)S(1)} %copy-done, s32[8,128]{1,0:T(8,128)S(1)} %copy-done.3, f32[8,128]{1,0:T(8,128)S(1)} %copy-done.4, f32[128,256]{1,0:T(8,128)S(1)} %get-tuple-element.36.own_ref, f32[8,128]{1,0:T(8,128)S(1)} %get-tuple-element.37.count_ref, ...), custom_call_target="tpu_custom_call" | custom-call | tf_op jit(solution)/shard_map/final_sum/pallas_call | solution.py:308
  (1 shorter events, 0.0 us)
Async XLA Ops:
  7.2 52.9 %all-gather.2.cloned.1.call-start = ((), (), s32[]{:S(2)}) async-start(), calls=%async_computation | async-start | bytes 4718592 | tf_op jit(solution)/shard_map/all_gather | solution.py:332
  29.6 3.0 %collective-permute-start = (bf16[4,520,256]{2,1,0:T(8,128)(2,1)}, bf16[4,520,256]{2,1,0:T(8,128)(2,1)S(1)}, u32[]{:S(2)}, u32[]{:S(2)}) collective-permute-start(bf16[4,520,256]{2,1,0:T(8,128)(2,1)} %get-tuple-element.25), channel_id=1, source_target_pairs={{0,1},{1,0},{2,3},{3,2},{4,5},{5,4},{6,7},{7,6},{8,9},{9,8},{10,11... | collective-permute-start | bytes 3194888 | tf_op jit(solution)/shard_map/ppermute | solution.py:324
  32.7 1.6 %copy-start.1 = (f32[4,512,256]{2,1,0:T(8,128)S(1)}, f32[4,512,256]{2,1,0:T(8,128)}, u32[]{:S(2)}) copy-start(f32[4,512,256]{2,1,0:T(8,128)} %get-tuple-element.23.keep_ref) | copy-start | bytes 6291460
  34.3 0.7 copy-start.2
  35.3 10.4 %collective-permute-start.1 = (bf16[4,136,256]{2,1,0:T(8,128)(2,1)S(1)}, bf16[4,136,256]{2,1,0:T(8,128)(2,1)S(1)}, u32[]{:S(2)}, u32[]{:S(2)}) collective-permute-start(bf16[4,136,256]{2,1,0:T(8,128)(2,1)S(1)} %get-tuple-element.28), channel_id=1, source_target_pairs={{0,8},{8,0},{16,24},{24,16},{1,9},{9,1},{17,25},{25,17},{2,10},{10... | collective-permute-start | bytes 835592 | tf_op jit(solution)/shard_map/ppermute | solution.py:324
  38.2 14.4 %collective-permute-start.2 = (bf16[4,136,256]{2,1,0:T(8,128)(2,1)S(1)}, bf16[4,136,256]{2,1,0:T(8,128)(2,1)S(1)}, u32[]{:S(2)}, u32[]{:S(2)}) collective-permute-start(bf16[4,136,256]{2,1,0:T(8,128)(2,1)S(1)} %get-tuple-element.29), channel_id=1, source_target_pairs={{0,16},{8,24},{16,0},{24,8},{1,17},{9,25},{17,1},{25,9},{2,18},{10... | collective-permute-start | bytes 835592 | tf_op jit(solution)/shard_map/ppermute | solution.py:324
  39.7 12.9 %collective-permute-start.3 = (bf16[4,136,256]{2,1,0:T(8,128)(2,1)S(1)}, bf16[4,136,256]{2,1,0:T(8,128)(2,1)S(1)}, u32[]{:S(2)}, u32[]{:S(2)}) collective-permute-start(bf16[4,136,256]{2,1,0:T(8,128)(2,1)S(1)} %get-tuple-element.30), channel_id=1, source_target_pairs={{0,24},{8,16},{16,8},{24,0},{1,25},{9,17},{17,9},{25,1},{2,26},{10... | collective-permute-start | bytes 835592 | tf_op jit(solution)/shard_map/ppermute | solution.py:324
  52.7 15.4 %collective-permute-start.4 = (bf16[136,256]{1,0:T(8,128)(2,1)S(1)}, bf16[136,256]{1,0:T(8,128)(2,1)S(1)}, u32[]{:S(2)}, u32[]{:S(2)}) collective-permute-start(bf16[136,256]{1,0:T(8,128)(2,1)S(1)} %get-tuple-element.31), channel_id=1, source_target_pairs={{0,2},{1,3},{2,0},{3,1},{4,6},{5,7},{6,4},{7,5},{8,10},{9,11},{10,... | collective-permute-start | bytes 208904 | tf_op jit(solution)/shard_map/ppermute | solution.py:324
  54.4 13.7 %collective-permute-start.5 = (bf16[136,256]{1,0:T(8,128)(2,1)S(1)}, bf16[136,256]{1,0:T(8,128)(2,1)S(1)}, u32[]{:S(2)}, u32[]{:S(2)}) collective-permute-start(bf16[136,256]{1,0:T(8,128)(2,1)S(1)} %get-tuple-element.32), channel_id=1, source_target_pairs={{0,4},{1,5},{2,6},{3,7},{4,0},{5,1},{6,2},{7,3},{8,12},{9,13},{10,... | collective-permute-start | bytes 208904 | tf_op jit(solution)/shard_map/ppermute | solution.py:324
  57.2 10.9 %collective-permute-start.6 = (bf16[136,256]{1,0:T(8,128)(2,1)S(1)}, bf16[136,256]{1,0:T(8,128)(2,1)S(1)}, u32[]{:S(2)}, u32[]{:S(2)}) collective-permute-start(bf16[136,256]{1,0:T(8,128)(2,1)S(1)} %get-tuple-element.33), channel_id=1, source_target_pairs={{0,6},{1,7},{2,4},{3,5},{4,2},{5,3},{6,0},{7,1},{8,14},{9,15},{10,... | collective-permute-start | bytes 208904 | tf_op jit(solution)/shard_map/ppermute | solution.py:324
  60.0 8.1 %copy-start = (f32[16,128,256]{2,1,0:T(8,128)S(1)}, f32[16,128,256]{2,1,0:T(8,128)}, u32[]{:S(2)}) copy-start(f32[16,128,256]{2,1,0:T(8,128)} %ctf_ref.3) | copy-start | bytes 6291460
  60.0 8.1 %copy-start.3 = (s32[8,128]{1,0:T(8,128)S(1)}, s32[8,128]{1,0:T(8,128)}, u32[]{:S(2)}) copy-start(s32[8,128]{1,0:T(8,128)} %slot_ref.3) | copy-start | bytes 12292
  60.0 8.2 %copy-start.4 = (f32[8,128]{1,0:T(8,128)S(1)}, f32[8,128]{1,0:T(8,128)}, u32[]{:S(2)}) copy-start(f32[8,128]{1,0:T(8,128)} %wt_ref.3) | copy-start | bytes 12292
Sparse Core Ops, SparseCore 0:
  9.6 50.3 all-gather.1

commit v2 on v1

--- a/solution.py
+++ b/solution.py
@@ -108,9 +108,10 @@
     return pl.pallas_call(
         functools.partial(front_kernel, blocks),
         grid_spec=pltpu.PrefetchScalarGridSpec(
-            num_scalar_prefetch=3,
+            num_scalar_prefetch=0,
             grid=(blocks + groups,),
             in_specs=[
+                *[pl.BlockSpec((number,), lambda i: (0,), memory_space=pltpu.SMEM)] * 3,
                 pl.BlockSpec((BLOCK, pixels, pixels), lambda i, *_: (at_block(i), 0, 0)),
                 whole((2, pixels, pixels)),
                 whole((bin_count, rows, pixels)),
@@ -133,59 +134,87 @@
             ],
         ),
         out_shape=[
-            jax.ShapeDtypeStruct((rows, number, pixels), jnp.bfloat16),
+            pltpu.HBM((rows, number, pixels), jnp.bfloat16),
             jax.ShapeDtypeStruct((groups, SLOTS, pixels), jnp.float32),
             jax.ShapeDtypeStruct((groups, SLOTS + orients, pixels), jnp.bfloat16),
             jax.ShapeDtypeStruct((groups, orients, pixels // 2), jnp.float32),
         ],
-        compiler_params=pltpu.CompilerParams(vmem_limit_bytes=60 * 2**20),
+        compiler_params=pltpu.CompilerParams(vmem_limit_bytes=40 * 2**20),
         cost_estimate=pl.CostEstimate(
             flops=8 * number * pixels**3, bytes_accessed=number * pixels**2 * 4, transcendentals=0
         ),
         name="front",
-    )(class_ids, orient_ids, bins, images, dft_tables(pixels), ctf_table, slice_slots, slot_weight)
-
-
-def score_kernel(w_ref, panel_ref, best_ref, acc):
+    )(
+        *(
+            pltpu.with_memory_space_constraint(x, pltpu.HBM)
+            for x in (
+                class_ids, orient_ids, bins, images, dft_tables(pixels), ctf_table, slice_slots, slot_weight,
+            )
+        )
+    )
+
+
+def score_kernel(orients, last, sum_ref, w_ref, *refs):
+    panels, (out_ref, even, odd) = refs[:-3], refs[-3:]
     step = pl.program_id(0)
+    number, pixels = w_ref.shape[1], w_ref.shape[2]
 
     @pl.when(step == 0)
     def _():
-        acc[...] = jnp.zeros_like(acc)
-
-    total = acc[...]
-    for j in range(w_ref.shape[0]):
-        panel = [panel_ref[c, j] for c in range(panel_ref.shape[0])]
-        total = total + lax.dot_general(
-            jnp.concatenate(panel, axis=0),
-            w_ref[j],
-            (((1,), (1,)), ((), ())),
-            preferred_element_type=jnp.float32,
+        even[...] = sum_ref[0]
+        odd[...] = sum_ref[1]
+
+    if len(panels) == 2:
+        blocks = [(ref, c) for ref in panels for c in range(ref.shape[0])]
+    else:
+        z, core = lax.axis_index("cls") // 2, lax.axis_index("cls") % 2
+        groups = range(panels[0].shape[0] // 2)
+        blocks = [(panels[0], 2 * (z ^ m) + c) for c in (core, 1 - core) for m in groups]
+    totals = [even[...], odd[...]]
+    for pair in range(w_ref.shape[0] // 2):
+        rows = pl.ds(pair * 2 * orients, 2 * orients)
+        both = jnp.concatenate([ref[c, rows, :] for ref, c in blocks], axis=0)
+        images = w_ref[2 * pair : 2 * pair + 2].reshape(2 * number, pixels)
+        scores = lax.dot_general(
+            images, both, (((1,), (1,)), ((), ())), preferred_element_type=jnp.float32
         )
-    acc[...] = total
+        totals = [totals[0] + scores[:number], totals[1] + scores[number:]]
+    even[...], odd[...] = totals
 
     @pl.when(step == pl.num_programs(0) - 1)
     def _():
-        scale = 1.0 / math.sqrt(pl.num_programs(0) * w_ref.shape[0] * w_ref.shape[2])
-        best_ref[...] = jnp.max(acc[...] * scale, axis=0, keepdims=True)
-
-
-def score(w2, panel, depth=16):
-    rows, number, pixels = w2.shape
-    classes, orients = panel.shape[0], panel.shape[2]
+        if last is None:
+            out_ref[0] = even[...]
+            out_ref[1] = odd[...]
+        else:
+            halves = (-1, 2, orients, number)
+            sums = jnp.transpose(even[...]).reshape(halves)[:, 0]
+            sums = (sums + jnp.transpose(odd[...]).reshape(halves)[:, 1]) * last
+            out_ref[...] = jnp.max(jnp.max(sums, axis=0), axis=0, keepdims=True)
+
+
+def score(w2, panels, sums, first, last=None, depth=32):
+    number, pixels = w2.shape[1], w2.shape[2]
+    orients = 8
+    steps = panels[0].shape[1] // (depth * orients)
+    hbm = lambda x: pltpu.with_memory_space_constraint(x, pltpu.HBM)
+    whole = lambda shape: pl.BlockSpec(shape, lambda i: (0,) * len(shape))
+    out_shape = sums.shape if last is None else (1, number)
     return pl.pallas_call(
-        score_kernel,
-        grid=(rows // depth,),
-        in_specs=[
-            pl.BlockSpec((depth, number, pixels), lambda i: (i, 0, 0)),
-            pl.BlockSpec((classes, depth, orients, pixels), lambda i: (0, i, 0, 0)),
+        functools.partial(score_kernel, orients, last),
+        grid=(steps,),
+        in_specs=[whole(sums.shape)]
+        + [pl.BlockSpec((depth, number, pixels), lambda i: (first // depth + i, 0, 0))]
+        + [
+            pl.BlockSpec((panel.shape[0], depth * orients, pixels), lambda i: (0, i, 0))
+            for panel in panels
         ],
-        out_specs=pl.BlockSpec((1, number), lambda i: (0, 0)),
-        scratch_shapes=[pltpu.VMEM((classes * orients, number), jnp.float32)],
-        out_shape=jax.ShapeDtypeStruct((1, number), jnp.float32),
-        compiler_params=pltpu.CompilerParams(vmem_limit_bytes=60 * 2**20),
+        out_specs=whole(out_shape),
+        scratch_shapes=[pltpu.VMEM(sums.shape[1:], jnp.float32)] * 2,
+        out_shape=jax.ShapeDtypeStruct(out_shape, jnp.float32),
+        compiler_params=pltpu.CompilerParams(vmem_limit_bytes=20 * 2**20),
         name="score",
-    )(w2, panel)
+    )(sums, hbm(w2), *(hbm(panel) for panel in panels))
 
 
 def chip_kernel(masks, keep_ref, count_ref, got_ref, own_ref, own_count_ref, *outs):
@@ -328,8 +357,13 @@
     images, ctf_table, defocus_bin, projections, best_class, best_orient, slice_slots, slot_weight
 ):
     classes, imgs = lax.axis_size("cls"), lax.axis_size("img")
-    own_panel = jnp.transpose(projections, (0, 2, 1, 3))
-    panel = lax.all_gather(own_panel, "cls", axis=0, tiled=True)
+    groups = classes // 2
+    rows, pixels = ctf_table.shape[1], images.shape[2]
+    orients = slot_weight.shape[0]
+    near_rows = rows * 1 // 2
+    own_panel = jnp.transpose(projections, (0, 2, 1, 3)).reshape(1, -1, pixels)
+    near = own_panel[:, : near_rows * orients]
+    near = [near] + [swap(near, "cls", 2 * m) for m in range(1, groups)]
     w2, keep, send, count = front(
         images,
         ctf_table,
@@ -340,12 +374,22 @@
         slot_weight,
         classes,
     )
+    send, near = lax.optimization_barrier((send, near))
     got = swap(send, "cls", 1)
     own, own_count, *parts = chip_sum(keep, count, got, imgs)
     gots = [swap(part, "img", m + 1) for m, part in enumerate(parts)]
+    far = own_panel[:, near_rows * orients :]
+    far = [far] + [swap(far, "cls", 2 * m) for m in range(1, groups)]
+    near = jnp.concatenate(near, axis=0)
+    other = swap(near, "cls", 1)
+    sums = jnp.zeros((2, images.shape[0], 2 * classes * orients), jnp.float32)
+    sums = score(w2, [near, other], sums, 0)
+    gots, sums = lax.optimization_barrier((gots, sums))
     data, data_count, *parts = plane_sum(own, own_count, gots)
     gots = [swap(part, "cls", 2 * (m + 1)) for m, part in enumerate(parts)]
-    best = score(w2, panel)
+    _, far = lax.optimization_barrier((data, far))
+    far = jnp.concatenate(far, axis=0)
+    best = score(w2, [far, swap(far, "cls", 1)], sums, near_rows, 1.0 / math.sqrt(rows * pixels))
     gots, best = lax.optimization_barrier((gots, best))
     data, weight = final_sum(ctf_table, slice_slots, slot_weight, data, data_count, gots)
     return (best.reshape(-1), data[None], weight[None])

time: 78.1 us -> 75.2 us (0.963)
  starting transfers between devices: 9.49 us -> 26.1 us
  between operations: 14.1 us -> 0.82 us
  Pallas kernels: 31.3 us -> 28.9 us
  local copies, waits for them, and re-layouts: 4.5 us -> 2.64 us
  waiting for transfers between devices: 18.2 us -> 16.4 us
    ppermute x7 -> x15, starting transfers between devices: 9.45 us -> 26.1 us  [swap(): return lax.ppermute(value, axis, [(i, i ^ mask) for i in range(size)])]
    unnamed x11 -> x20, local copies, waits for them, and re-layouts: 4.5 us -> 1.22 us
    all_gather x1 -> x0, waiting for transfers between devices: 2.79 us -> none  [on_device(): panel = lax.all_gather(own_panel, 'cls', axis=0, tiled=True)]
    pallas_call x1 -> x2, Pallas kernels: 8.11 us -> 6.71 us  [score(): pl.pallas_call(functools.partial(score_kernel, orients, last), grid=(step...]
    transpose x0 -> x1, local copies, waits for them, and re-layouts: none -> 1.33 us  [on_device(): own_panel = jnp.transpose(projections, (0, 2, 1, 3)).reshape(1, -1, pixels)]
    pallas_call x1, Pallas kernels: 20.3 us -> 19.2 us  [front(): pl.pallas_call(functools.partial(front_kernel, blocks), grid_spec=pltpu.P...]
    ppermute x7 -> x15, waiting for transfers between devices: 15.4 us -> 16.4 us  [swap(): return lax.ppermute(value, axis, [(i, i ^ mask) for i in range(size)])]
  transfers between devices with their start and end apart: 8 -> 15, of which waited for: 4 -> 5; matrix products, arithmetic and copies ran while one was open for 0% -> 0% of each run, Pallas kernels for 37% -> 35%
where the time goes in v2:
time: 75.2 us; the launch traced here: 74.8 us
  Pallas kernels  28.9 us (38%)
  starting transfers between devices  26.1 us (35%)
  waiting for transfers between devices  16.4 us (22%)
  local copies, waits for them, and re-layouts  2.64 us (4%)
  between operations  0.82 us (1%)
    ppermute x15, starting transfers between devices, swap(): return lax.ppermute(value, axis, [(i, i ^ mask) for i in range(size)])  26.1 us
    pallas_call x1, Pallas kernels, front(): pl.pallas_call(functools.partial(front_kernel, blocks), grid_spec=pltpu.P...  19.2 us
    ppermute x15, waiting for transfers between devices, swap(): return lax.ppermute(value, axis, [(i, i ^ mask) for i in range(size)])  16.4 us
    pallas_call x2, Pallas kernels, score(): pl.pallas_call(functools.partial(score_kernel, orients, last), grid=(step...  6.71 us
    pallas_call x1, Pallas kernels, final_sum(): pl.pallas_call(final_kernel, in_specs=[vmem] * (5 + len(gots)), out_specs...  2.54 us
  transfers between devices with their start and end apart: 15, of which 5 were waited for; matrix products, arithmetic and copies ran while one was open for 0% of the time, Pallas kernels for 35%

profile of v2, /device:TPU:0, one launch (start us, length us, event | category | flops | bytes accessed | tf_op | source)
XLA Modules:
  0.0 74.8 jit_solution(452829837237080173)
XLA Ops:
  0.6 1.3 %copy.14 = bf16[1,128,8,256]{3,2,1,0:T(8,128)(2,1)S(1)} copy(bf16[1,128,8,256]{3,1,2,0:T(8,128)(2,1)} %bitcast.9) | data formatting | bytes 1048576 | tf_op jit(solution)/shard_map/transpose | solution.py:364
  2.0 3.1 %collective-permute-start = (bf16[1,512,256]{2,1,0:T(8,128)(2,1)S(1)}, bf16[1,512,256]{2,1,0:T(8,128)(2,1)S(1)}, u32[]{:S(2)}, u32[]{:S(2)}) collective-permute-start(bf16[1,512,256]{2,1,0:T(8,128)(2,1)S(1)} %get-tuple-element.46), channel_id=1, source_target_pairs={{0,2},{1,3},{2,0},{3,1},{4,6},{5,7},{6,4},{7,5},{8,10},{9,11},{10,... | collective-permute-start | bytes 786440 | tf_op jit(solution)/shard_map/ppermute | solution.py:353
  5.1 2.6 %collective-permute-start.1 = (bf16[1,512,256]{2,1,0:T(8,128)(2,1)S(1)}, bf16[1,512,256]{2,1,0:T(8,128)(2,1)S(1)}, u32[]{:S(2)}, u32[]{:S(2)}) collective-permute-start(bf16[1,512,256]{2,1,0:T(8,128)(2,1)S(1)} %get-tuple-element.46), channel_id=1, source_target_pairs={{0,4},{1,5},{2,6},{3,7},{4,0},{5,1},{6,2},{7,3},{8,12},{9,13},{10,... | collective-permute-start | bytes 786440 | tf_op jit(solution)/shard_map/ppermute | solution.py:353
  7.7 0.0 collective-permute-start.2
  7.7 19.2 %front.1 = (bf16[128,96,256]{2,1,0:T(8,128)(2,1)}, f32[4,512,256]{2,1,0:T(8,128)S(1)}, bf16[4,520,256]{2,1,0:T(8,128)(2,1)S(1)}, f32[4,8,128]{2,1,0:T(8,128)S(1)}) custom-call(s32[96]{0:T(128)} %bitcast.13, s32[96]{0:T(128)} %orient_ref.1, s32[96]{0:T(128)} %bin_ref.1, bf16[96,256,256]{2,1,0:T(8,128)(2,1)} %img_ref.1, ...), custom_call_target="tpu_custom_call" | custom-call | flops 12884901888 | bytes 25165824 | tf_op jit(solution)/shard_map/front/pallas_call | solution.py:108
  26.9 0.0 collective-permute-done.2
  26.9 0.1 collective-permute-start.3
  27.1 0.6 collective-permute-start.7
  27.7 2.0 %collective-permute-done.3.got_ref = bf16[4,520,256]{2,1,0:T(8,128)(2,1)S(1)} collective-permute-done((bf16[4,520,256]{2,1,0:T(8,128)(2,1)S(1)}, bf16[4,520,256]{2,1,0:T(8,128)(2,1)S(1)}, u32[]{:S(2)}, u32[]{:S(2)}) %collective-permute-start.3) | collective-permute-done | bytes 1064992 | tf_op jit(solution)/shard_map/ppermute | solution.py:353
  29.7 0.3 chip_sum.1
  30.0 1.7 %collective-permute-start.4 = (bf16[4,136,256]{2,1,0:T(8,128)(2,1)S(1)}, bf16[4,136,256]{2,1,0:T(8,128)(2,1)S(1)}, u32[]{:S(2)}, u32[]{:S(2)}) collective-permute-start(bf16[4,136,256]{2,1,0:T(8,128)(2,1)S(1)} %get-tuple-element.42), channel_id=1, source_target_pairs={{0,8},{8,0},{16,24},{24,16},{1,9},{9,1},{17,25},{25,17},{2,10},{10... | collective-permute-start | bytes 835592 | tf_op jit(solution)/shard_map/ppermute | solution.py:353
  31.7 1.5 %collective-permute-start.5 = (bf16[4,136,256]{2,1,0:T(8,128)(2,1)S(1)}, bf16[4,136,256]{2,1,0:T(8,128)(2,1)S(1)}, u32[]{:S(2)}, u32[]{:S(2)}) collective-permute-start(bf16[4,136,256]{2,1,0:T(8,128)(2,1)S(1)} %get-tuple-element.43), channel_id=1, source_target_pairs={{0,16},{8,24},{16,0},{24,8},{1,17},{9,25},{17,1},{25,9},{2,18},{10... | collective-permute-start | bytes 835592 | tf_op jit(solution)/shard_map/ppermute | solution.py:353
  33.2 0.3 collective-permute-start.6
  33.5 4.2 %collective-permute-start.11 = (bf16[1,512,256]{2,1,0:T(8,128)(2,1)S(1)}, bf16[1,512,256]{2,1,0:T(8,128)(2,1)S(1)}, u32[]{:S(2)}, u32[]{:S(2)}) collective-permute-start(bf16[1,512,256]{2,1,0:T(8,128)(2,1)S(1)} %get-tuple-element.58), channel_id=1, source_target_pairs={{0,2},{1,3},{2,0},{3,1},{4,6},{5,7},{6,4},{7,5},{8,10},{9,11},{10,... | collective-permute-start | bytes 786440 | tf_op jit(solution)/shard_map/ppermute | solution.py:353
  37.8 0.0 collective-permute-done.7.refs_1_
  37.8 1.1 %collective-permute-start.12 = (bf16[1,512,256]{2,1,0:T(8,128)(2,1)S(1)}, bf16[1,512,256]{2,1,0:T(8,128)(2,1)S(1)}, u32[]{:S(2)}, u32[]{:S(2)}) collective-permute-start(bf16[1,512,256]{2,1,0:T(8,128)(2,1)S(1)} %get-tuple-element.58), channel_id=1, source_target_pairs={{0,4},{1,5},{2,6},{3,7},{4,0},{5,1},{6,2},{7,3},{8,12},{9,13},{10,... | collective-permute-start | bytes 786440 | tf_op jit(solution)/shard_map/ppermute | solution.py:353
  38.9 0.7 collective-permute-done.4.refs_0_
  39.5 3.8 %collective-permute-start.13 = (bf16[1,512,256]{2,1,0:T(8,128)(2,1)S(1)}, bf16[1,512,256]{2,1,0:T(8,128)(2,1)S(1)}, u32[]{:S(2)}, u32[]{:S(2)}) collective-permute-start(bf16[1,512,256]{2,1,0:T(8,128)(2,1)S(1)} %get-tuple-element.58), channel_id=1, source_target_pairs={{0,6},{1,7},{2,4},{3,5},{4,2},{5,3},{6,0},{7,1},{8,14},{9,15},{10,... | collective-permute-start | bytes 786440 | tf_op jit(solution)/shard_map/ppermute | solution.py:353
  43.4 3.1 %score.2.sum_ref = f32[2,96,128]{2,1,0:T(8,128)S(1)} custom-call(f32[2,96,128]{2,1,0:T(8,128)S(1)} %broadcast_in_dim.9.sum_ref, bf16[128,96,256]{2,1,0:T(8,128)(2,1)} %get-tuple-element.45.w_ref, bf16[4,512,256]{2,1,0:T(8,128)(2,1)} %copy-done.4, bf16[4,512,256]{2,1,0:T(8,128)(2,1)} %copy-done.6), custom_call_target="tpu_custom_call" | custom-call | tf_op jit(solution)/shard_map/score/pallas_call | solution.py:203
  46.4 0.0 collective-permute-done.5.refs_1_
  46.4 0.0 collective-permute-done.6.refs_2_
  46.5 0.2 plane_sum.1
  46.6 1.6 %collective-permute-done.11 = bf16[1,512,256]{2,1,0:T(8,128)(2,1)S(1)} collective-permute-done((bf16[1,512,256]{2,1,0:T(8,128)(2,1)S(1)}, bf16[1,512,256]{2,1,0:T(8,128)(2,1)S(1)}, u32[]{:S(2)}, u32[]{:S(2)}) %collective-permute-start.11) | collective-permute-done | bytes 262176 | tf_op jit(solution)/shard_map/ppermute | solution.py:353
  48.2 10.7 %collective-permute-done.12 = bf16[1,512,256]{2,1,0:T(8,128)(2,1)S(1)} collective-permute-done((bf16[1,512,256]{2,1,0:T(8,128)(2,1)S(1)}, bf16[1,512,256]{2,1,0:T(8,128)(2,1)S(1)}, u32[]{:S(2)}, u32[]{:S(2)}) %collective-permute-start.12) | collective-permute-done | bytes 262176 | tf_op jit(solution)/shard_map/ppermute | solution.py:353
  59.0 0.1 collective-permute-start.14
  59.1 4.5 %collective-permute-start.8 = (bf16[136,256]{1,0:T(8,128)(2,1)S(1)}, bf16[136,256]{1,0:T(8,128)(2,1)S(1)}, u32[]{:S(2)}, u32[]{:S(2)}) collective-permute-start(bf16[136,256]{1,0:T(8,128)(2,1)S(1)} %get-tuple-element.53), channel_id=1, source_target_pairs={{0,2},{1,3},{2,0},{3,1},{4,6},{5,7},{6,4},{7,5},{8,10},{9,11},{10,... | collective-permute-start | bytes 208904 | tf_op jit(solution)/shard_map/ppermute | solution.py:353
  63.6 1.1 %collective-permute-start.9 = (bf16[136,256]{1,0:T(8,128)(2,1)S(1)}, bf16[136,256]{1,0:T(8,128)(2,1)S(1)}, u32[]{:S(2)}, u32[]{:S(2)}) collective-permute-start(bf16[136,256]{1,0:T(8,128)(2,1)S(1)} %get-tuple-element.54), channel_id=1, source_target_pairs={{0,4},{1,5},{2,6},{3,7},{4,0},{5,1},{6,2},{7,3},{8,12},{9,13},{10,... | collective-permute-start | bytes 208904 | tf_op jit(solution)/shard_map/ppermute | solution.py:353
  64.7 1.5 %collective-permute-start.10 = (bf16[136,256]{1,0:T(8,128)(2,1)S(1)}, bf16[136,256]{1,0:T(8,128)(2,1)S(1)}, u32[]{:S(2)}, u32[]{:S(2)}) collective-permute-start(bf16[136,256]{1,0:T(8,128)(2,1)S(1)} %get-tuple-element.55), channel_id=1, source_target_pairs={{0,6},{1,7},{2,4},{3,5},{4,2},{5,3},{6,0},{7,1},{8,14},{9,15},{10,... | collective-permute-start | bytes 208904 | tf_op jit(solution)/shard_map/ppermute | solution.py:353
  66.2 1.1 %copy-done.5 = bf16[4,512,256]{2,1,0:T(8,128)(2,1)} copy-done((bf16[4,512,256]{2,1,0:T(8,128)(2,1)}, bf16[4,512,256]{2,1,0:T(8,128)(2,1)S(1)}, u32[]{:S(2)}) %copy-start.5) | copy-done | bytes 1048600
  67.3 3.6 %score.3 = f32[1,96]{1,0:T(1,128)} custom-call(f32[2,96,128]{2,1,0:T(8,128)S(1)} %score.2.sum_ref, bf16[128,96,256]{2,1,0:T(8,128)(2,1)} %get-tuple-element.45.w_ref, bf16[4,512,256]{2,1,0:T(8,128)(2,1)} %copy-done.3, bf16[4,512,256]{2,1,0:T(8,128)(2,1)} %copy-done.5), custom_call_target="tpu_custom_call" | custom-call | tf_op jit(solution)/shard_map/score/pallas_call | solution.py:203
  70.9 1.4 %collective-permute-done.9.refs_1_ = bf16[136,256]{1,0:T(8,128)(2,1)S(1)} collective-permute-done((bf16[136,256]{1,0:T(8,128)(2,1)S(1)}, bf16[136,256]{1,0:T(8,128)(2,1)S(1)}, u32[]{:S(2)}, u32[]{:S(2)}) %collective-permute-start.9) | collective-permute-done | bytes 69664 | tf_op jit(solution)/shard_map/ppermute | solution.py:353
  72.3 2.5 %final_sum.1 = (f32[128,256]{1,0:T(8,128)}, f32[128,256]{1,0:T(8,128)}) custom-call(f32[16,128,256]{2,1,0:T(8,128)S(1)} %copy-done, s32[8,128]{1,0:T(8,128)S(1)} %copy-done.1, f32[8,128]{1,0:T(8,128)S(1)} %copy-done.2, f32[128,256]{1,0:T(8,128)S(1)} %get-tuple-element.57.own_ref, f32[8,128]{1,0:T(8,128)S(1)} %get-tuple-element.63.count_ref, ...), custom_call_target="tpu_custom_call" | custom-call | tf_op jit(solution)/shard_map/final_sum/pallas_call | solution.py:337
  (29 shorter events, 0.2 us)
Async XLA Ops:
  2.0 24.9 %collective-permute-start = (bf16[1,512,256]{2,1,0:T(8,128)(2,1)S(1)}, bf16[1,512,256]{2,1,0:T(8,128)(2,1)S(1)}, u32[]{:S(2)}, u32[]{:S(2)}) collective-permute-start(bf16[1,512,256]{2,1,0:T(8,128)(2,1)S(1)} %get-tuple-element.46), channel_id=1, source_target_pairs={{0,2},{1,3},{2,0},{3,1},{4,6},{5,7},{6,4},{7,5},{8,10},{9,11},{10,... | collective-permute-start | bytes 786440 | tf_op jit(solution)/shard_map/ppermute | solution.py:353
  5.1 21.8 %collective-permute-start.1 = (bf16[1,512,256]{2,1,0:T(8,128)(2,1)S(1)}, bf16[1,512,256]{2,1,0:T(8,128)(2,1)S(1)}, u32[]{:S(2)}, u32[]{:S(2)}) collective-permute-start(bf16[1,512,256]{2,1,0:T(8,128)(2,1)S(1)} %get-tuple-element.46), channel_id=1, source_target_pairs={{0,4},{1,5},{2,6},{3,7},{4,0},{5,1},{6,2},{7,3},{8,12},{9,13},{10,... | collective-permute-start | bytes 786440 | tf_op jit(solution)/shard_map/ppermute | solution.py:353
  7.7 19.2 %collective-permute-start.2 = (bf16[1,512,256]{2,1,0:T(8,128)(2,1)S(1)}, bf16[1,512,256]{2,1,0:T(8,128)(2,1)S(1)}, u32[]{:S(2)}, u32[]{:S(2)}) collective-permute-start(bf16[1,512,256]{2,1,0:T(8,128)(2,1)S(1)} %get-tuple-element.46), channel_id=1, source_target_pairs={{0,6},{1,7},{2,4},{3,5},{4,2},{5,3},{6,0},{7,1},{8,14},{9,15},{10,... | collective-permute-start | bytes 786440 | tf_op jit(solution)/shard_map/ppermute | solution.py:353
  26.9 2.7 %collective-permute-start.3 = (bf16[4,520,256]{2,1,0:T(8,128)(2,1)S(1)}, bf16[4,520,256]{2,1,0:T(8,128)(2,1)S(1)}, u32[]{:S(2)}, u32[]{:S(2)}) collective-permute-start(bf16[4,520,256]{2,1,0:T(8,128)(2,1)S(1)} %get-tuple-element.39), channel_id=1, source_target_pairs={{0,1},{1,0},{2,3},{3,2},{4,5},{5,4},{6,7},{7,6},{8,9},{9,8},{10,11... | collective-permute-start | bytes 3194888 | tf_op jit(solution)/shard_map/ppermute | solution.py:353
  27.1 16.2 %copy-start.4 = (bf16[4,512,256]{2,1,0:T(8,128)(2,1)}, bf16[4,512,256]{2,1,0:T(8,128)(2,1)S(1)}, u32[]{:S(2)}) copy-start(bf16[4,512,256]{2,1,0:T(8,128)(2,1)S(1)} %constant_dynamic-update-slice_fusion.refs_0_) | copy-start | bytes 3145732
  27.1 10.6 %collective-permute-start.7 = (bf16[4,512,256]{2,1,0:T(8,128)(2,1)S(1)}, bf16[4,512,256]{2,1,0:T(8,128)(2,1)S(1)}, u32[]{:S(2)}, u32[]{:S(2)}) collective-permute-start(bf16[4,512,256]{2,1,0:T(8,128)(2,1)S(1)} %constant_dynamic-update-slice_fusion.refs_0_), channel_id=1, source_target_pairs={{0,1},{1,0},{2,3},{3,2},{4,5},{5,4},{6,7},{7,6},{8,9},{9,8},{10,11... | collective-permute-start | bytes 3145736 | tf_op jit(solution)/shard_map/ppermute | solution.py:353
  30.0 9.6 %collective-permute-start.4 = (bf16[4,136,256]{2,1,0:T(8,128)(2,1)S(1)}, bf16[4,136,256]{2,1,0:T(8,128)(2,1)S(1)}, u32[]{:S(2)}, u32[]{:S(2)}) collective-permute-start(bf16[4,136,256]{2,1,0:T(8,128)(2,1)S(1)} %get-tuple-element.42), channel_id=1, source_target_pairs={{0,8},{8,0},{16,24},{24,16},{1,9},{9,1},{17,25},{25,17},{2,10},{10... | collective-permute-start | bytes 835592 | tf_op jit(solution)/shard_map/ppermute | solution.py:353
  31.7 14.7 %collective-permute-start.5 = (bf16[4,136,256]{2,1,0:T(8,128)(2,1)S(1)}, bf16[4,136,256]{2,1,0:T(8,128)(2,1)S(1)}, u32[]{:S(2)}, u32[]{:S(2)}) collective-permute-start(bf16[4,136,256]{2,1,0:T(8,128)(2,1)S(1)} %get-tuple-element.43), channel_id=1, source_target_pairs={{0,16},{8,24},{16,0},{24,8},{1,17},{9,25},{17,1},{25,9},{2,18},{10... | collective-permute-start | bytes 835592 | tf_op jit(solution)/shard_map/ppermute | solution.py:353
  33.2 13.2 %collective-permute-start.6 = (bf16[4,136,256]{2,1,0:T(8,128)(2,1)S(1)}, bf16[4,136,256]{2,1,0:T(8,128)(2,1)S(1)}, u32[]{:S(2)}, u32[]{:S(2)}) collective-permute-start(bf16[4,136,256]{2,1,0:T(8,128)(2,1)S(1)} %get-tuple-element.44), channel_id=1, source_target_pairs={{0,24},{8,16},{16,8},{24,0},{1,25},{9,17},{17,9},{25,1},{2,26},{10... | collective-permute-start | bytes 835592 | tf_op jit(solution)/shard_map/ppermute | solution.py:353
  33.5 14.7 %collective-permute-start.11 = (bf16[1,512,256]{2,1,0:T(8,128)(2,1)S(1)}, bf16[1,512,256]{2,1,0:T(8,128)(2,1)S(1)}, u32[]{:S(2)}, u32[]{:S(2)}) collective-permute-start(bf16[1,512,256]{2,1,0:T(8,128)(2,1)S(1)} %get-tuple-element.58), channel_id=1, source_target_pairs={{0,2},{1,3},{2,0},{3,1},{4,6},{5,7},{6,4},{7,5},{8,10},{9,11},{10,... | collective-permute-start | bytes 786440 | tf_op jit(solution)/shard_map/ppermute | solution.py:353
  37.8 5.6 %copy-start.6 = (bf16[4,512,256]{2,1,0:T(8,128)(2,1)}, bf16[4,512,256]{2,1,0:T(8,128)(2,1)S(1)}, u32[]{:S(2)}) copy-start(bf16[4,512,256]{2,1,0:T(8,128)(2,1)S(1)} %collective-permute-done.7.refs_1_) | copy-start | bytes 3145732
  37.8 21.1 %collective-permute-start.12 = (bf16[1,512,256]{2,1,0:T(8,128)(2,1)S(1)}, bf16[1,512,256]{2,1,0:T(8,128)(2,1)S(1)}, u32[]{:S(2)}, u32[]{:S(2)}) collective-permute-start(bf16[1,512,256]{2,1,0:T(8,128)(2,1)S(1)} %get-tuple-element.58), channel_id=1, source_target_pairs={{0,4},{1,5},{2,6},{3,7},{4,0},{5,1},{6,2},{7,3},{8,12},{9,13},{10,... | collective-permute-start | bytes 786440 | tf_op jit(solution)/shard_map/ppermute | solution.py:353
  39.5 19.4 %collective-permute-start.13 = (bf16[1,512,256]{2,1,0:T(8,128)(2,1)S(1)}, bf16[1,512,256]{2,1,0:T(8,128)(2,1)S(1)}, u32[]{:S(2)}, u32[]{:S(2)}) collective-permute-start(bf16[1,512,256]{2,1,0:T(8,128)(2,1)S(1)} %get-tuple-element.58), channel_id=1, source_target_pairs={{0,6},{1,7},{2,4},{3,5},{4,2},{5,3},{6,0},{7,1},{8,14},{9,15},{10,... | collective-permute-start | bytes 786440 | tf_op jit(solution)/shard_map/ppermute | solution.py:353
  59.0 7.2 %copy-start.3 = (bf16[4,512,256]{2,1,0:T(8,128)(2,1)}, bf16[4,512,256]{2,1,0:T(8,128)(2,1)S(1)}, u32[]{:S(2)}) copy-start(bf16[4,512,256]{2,1,0:T(8,128)(2,1)S(1)} %constant_dynamic-update-slice_fusion.4.refs_0_) | copy-start | bytes 3145732
  59.0 7.1 %collective-permute-start.14 = (bf16[4,512,256]{2,1,0:T(8,128)(2,1)S(1)}, bf16[4,512,256]{2,1,0:T(8,128)(2,1)S(1)}, u32[]{:S(2)}, u32[]{:S(2)}) collective-permute-start(bf16[4,512,256]{2,1,0:T(8,128)(2,1)S(1)} %constant_dynamic-update-slice_fusion.4.refs_0_), channel_id=1, source_target_pairs={{0,1},{1,0},{2,3},{3,2},{4,5},{5,4},{6,7},{7,6},{8,9},{9,8},{10,11... | collective-permute-start | bytes 3145736 | tf_op jit(solution)/shard_map/ppermute | solution.py:353
  59.1 11.8 %collective-permute-start.8 = (bf16[136,256]{1,0:T(8,128)(2,1)S(1)}, bf16[136,256]{1,0:T(8,128)(2,1)S(1)}, u32[]{:S(2)}, u32[]{:S(2)}) collective-permute-start(bf16[136,256]{1,0:T(8,128)(2,1)S(1)} %get-tuple-element.53), channel_id=1, source_target_pairs={{0,2},{1,3},{2,0},{3,1},{4,6},{5,7},{6,4},{7,5},{8,10},{9,11},{10,... | collective-permute-start | bytes 208904 | tf_op jit(solution)/shard_map/ppermute | solution.py:353
  63.6 8.7 %collective-permute-start.9 = (bf16[136,256]{1,0:T(8,128)(2,1)S(1)}, bf16[136,256]{1,0:T(8,128)(2,1)S(1)}, u32[]{:S(2)}, u32[]{:S(2)}) collective-permute-start(bf16[136,256]{1,0:T(8,128)(2,1)S(1)} %get-tuple-element.54), channel_id=1, source_target_pairs={{0,4},{1,5},{2,6},{3,7},{4,0},{5,1},{6,2},{7,3},{8,12},{9,13},{10,... | collective-permute-start | bytes 208904 | tf_op jit(solution)/shard_map/ppermute | solution.py:353
  64.7 7.6 %copy-start = (f32[16,128,256]{2,1,0:T(8,128)S(1)}, f32[16,128,256]{2,1,0:T(8,128)}, u32[]{:S(2)}) copy-start(f32[16,128,256]{2,1,0:T(8,128)} %ctf_ref.3) | copy-start | bytes 6291460
  64.7 7.6 %copy-start.1 = (s32[8,128]{1,0:T(8,128)S(1)}, s32[8,128]{1,0:T(8,128)}, u32[]{:S(2)}) copy-start(s32[8,128]{1,0:T(8,128)} %slot_ref.3) | copy-start | bytes 12292
  64.7 7.6 %copy-start.2 = (f32[8,128]{1,0:T(8,128)S(1)}, f32[8,128]{1,0:T(8,128)}, u32[]{:S(2)}) copy-start(f32[8,128]{1,0:T(8,128)} %wt_ref.3) | copy-start | bytes 12292
  64.7 7.6 %collective-permute-start.10 = (bf16[136,256]{1,0:T(8,128)(2,1)S(1)}, bf16[136,256]{1,0:T(8,128)(2,1)S(1)}, u32[]{:S(2)}, u32[]{:S(2)}) collective-permute-start(bf16[136,256]{1,0:T(8,128)(2,1)S(1)} %get-tuple-element.55), channel_id=1, source_target_pairs={{0,6},{1,7},{2,4},{3,5},{4,2},{5,3},{6,0},{7,1},{8,14},{9,15},{10,... | collective-permute-start | bytes 208904 | tf_op jit(solution)/shard_map/ppermute | solution.py:353
  66.2 1.1 %copy-start.5 = (bf16[4,512,256]{2,1,0:T(8,128)(2,1)}, bf16[4,512,256]{2,1,0:T(8,128)(2,1)S(1)}, u32[]{:S(2)}) copy-start(bf16[4,512,256]{2,1,0:T(8,128)(2,1)S(1)} %collective-permute-done.14.refs_1_) | copy-start | bytes 3145732

commit v3 on v2

--- a/solution.py
+++ b/solution.py
@@ -154,7 +154,7 @@
     )
 
 
-def score_kernel(orients, last, sum_ref, w_ref, *refs):
+def score_kernel(orients, last, first_ref, sum_ref, w_ref, *refs):
     panels, (out_ref, even, odd) = refs[:-3], refs[-3:]
     step = pl.program_id(0)
     number, pixels = w_ref.shape[1], w_ref.shape[2]
@@ -198,23 +198,28 @@
     orients = 8
     steps = panels[0].shape[1] // (depth * orients)
     hbm = lambda x: pltpu.with_memory_space_constraint(x, pltpu.HBM)
-    whole = lambda shape: pl.BlockSpec(shape, lambda i: (0,) * len(shape))
+    whole = lambda shape: pl.BlockSpec(shape, lambda i, first: (0,) * len(shape))
     out_shape = sums.shape if last is None else (1, number)
     return pl.pallas_call(
         functools.partial(score_kernel, orients, last),
-        grid=(steps,),
-        in_specs=[whole(sums.shape)]
-        + [pl.BlockSpec((depth, number, pixels), lambda i: (first // depth + i, 0, 0))]
-        + [
-            pl.BlockSpec((panel.shape[0], depth * orients, pixels), lambda i: (0, i, 0))
-            for panel in panels
-        ],
-        out_specs=whole(out_shape),
-        scratch_shapes=[pltpu.VMEM(sums.shape[1:], jnp.float32)] * 2,
+        grid_spec=pltpu.PrefetchScalarGridSpec(
+            num_scalar_prefetch=1,
+            grid=(steps,),
+            in_specs=[
+                whole(sums.shape),
+                pl.BlockSpec((depth, number, pixels), lambda i, first: (first[0] * steps + i, 0, 0)),
+            ]
+            + [
+                pl.BlockSpec((panel.shape[0], depth * orients, pixels), lambda i, first: (0, i, 0))
+                for panel in panels
+            ],
+            out_specs=whole(out_shape),
+            scratch_shapes=[pltpu.VMEM(sums.shape[1:], jnp.float32)] * 2,
+        ),
         out_shape=jax.ShapeDtypeStruct(out_shape, jnp.float32),
         compiler_params=pltpu.CompilerParams(vmem_limit_bytes=20 * 2**20),
         name="score",
-    )(sums, hbm(w2), *(hbm(panel) for panel in panels))
+    )(first[None], sums, hbm(w2), *(hbm(panel) for panel in panels))
 
 
 def chip_kernel(masks, keep_ref, count_ref, got_ref, own_ref, own_count_ref, *outs):
@@ -362,8 +367,11 @@
     orients = slot_weight.shape[0]
     near_rows = rows * 1 // 2
     own_panel = jnp.transpose(projections, (0, 2, 1, 3)).reshape(1, -1, pixels)
-    near = own_panel[:, : near_rows * orients]
-    near = [near] + [swap(near, "cls", 2 * m) for m in range(1, groups)]
+    cut = near_rows * orients
+    my_img = lax.axis_index("img")
+    parity = (my_img ^ (my_img >> 1)) & 1
+    half = lambda p: lax.dynamic_slice_in_dim(own_panel, p * cut, cut, axis=1)
+    near = [swap(half(parity), "cls", 2 * m) for m in range(1, groups)]
     w2, keep, send, count = front(
         images,
         ctf_table,
@@ -378,18 +386,16 @@
     got = swap(send, "cls", 1)
     own, own_count, *parts = chip_sum(keep, count, got, imgs)
     gots = [swap(part, "img", m + 1) for m, part in enumerate(parts)]
-    far = own_panel[:, near_rows * orients :]
-    far = [far] + [swap(far, "cls", 2 * m) for m in range(1, groups)]
-    near = jnp.concatenate(near, axis=0)
+    near = jnp.concatenate([half(parity)] + near, axis=0)
+    far = [swap(near[1:, : cut // 2], "img", 1), swap(near[1:, cut // 2 :], "img", 2)]
     other = swap(near, "cls", 1)
     sums = jnp.zeros((2, images.shape[0], 2 * classes * orients), jnp.float32)
-    sums = score(w2, [near, other], sums, 0)
-    gots, sums = lax.optimization_barrier((gots, sums))
+    sums = score(w2, [near, other], sums, parity)
+    gots, sums, far = lax.optimization_barrier((gots, sums, far))
     data, data_count, *parts = plane_sum(own, own_count, gots)
     gots = [swap(part, "cls", 2 * (m + 1)) for m, part in enumerate(parts)]
-    _, far = lax.optimization_barrier((data, far))
-    far = jnp.concatenate(far, axis=0)
-    best = score(w2, [far, swap(far, "cls", 1)], sums, near_rows, 1.0 / math.sqrt(rows * pixels))
+    far = jnp.concatenate([half(1 - parity), jnp.concatenate(far, axis=1)], axis=0)
+    best = score(w2, [far, swap(far, "cls", 1)], sums, 1 - parity, 1.0 / math.sqrt(rows * pixels))
     gots, best = lax.optimization_barrier((gots, best))
     data, weight = final_sum(ctf_table, slice_slots, slot_weight, data, data_count, gots)
     return (best.reshape(-1), data[None], weight[None])

time: 75.2 us -> 68.3 us (0.908)
  starting transfers between devices: 26.1 us -> 19.8 us
  waiting for transfers between devices: 16.4 us -> 15.5 us
    ppermute x15 -> x14, starting transfers between devices: 26.1 us -> 19.8 us  [swap(): return lax.ppermute(value, axis, [(i, i ^ mask) for i in range(size)])]
    ppermute x15 -> x14, waiting for transfers between devices: 16.4 us -> 15.5 us  [swap(): return lax.ppermute(value, axis, [(i, i ^ mask) for i in range(size)])]
  transfers between devices with their start and end apart: 15 -> 14, of which waited for: 5 -> 5; matrix products, arithmetic and copies ran while one was open for 0% -> 0% of each run, Pallas kernels for 35% -> 39%
where the time goes in v3:
time: 68.3 us; the launch traced here: 68 us
  Pallas kernels  29.1 us (43%)
  starting transfers between devices  19.8 us (29%)
  waiting for transfers between devices  15.5 us (23%)
  local copies, waits for them, and re-layouts  2.6 us (4%)
  between operations  0.78 us (1%)
    ppermute x14, starting transfers between devices, swap(): return lax.ppermute(value, axis, [(i, i ^ mask) for i in range(size)])  19.8 us
    pallas_call x1, Pallas kernels, front(): pl.pallas_call(functools.partial(front_kernel, blocks), grid_spec=pltpu.P...  19.2 us
    ppermute x14, waiting for transfers between devices, swap(): return lax.ppermute(value, axis, [(i, i ^ mask) for i in range(size)])  15.5 us
    pallas_call x2, Pallas kernels, score(): pl.pallas_call(functools.partial(score_kernel, orients, last), grid_spec=...  6.89 us
    pallas_call x1, Pallas kernels, final_sum(): pl.pallas_call(final_kernel, in_specs=[vmem] * (5 + len(gots)), out_specs...  2.56 us
  transfers between devices with their start and end apart: 14, of which 5 were waited for; matrix products, arithmetic and copies ran while one was open for 0% of the time, Pallas kernels for 39%

profile of v3, /device:TPU:0, one launch (start us, length us, event | category | flops | bytes accessed | tf_op | source)
XLA Modules:
  0.0 68.0 jit_solution(5884203799320701797)
XLA Ops:
  0.6 1.3 %copy.14 = bf16[1,128,8,256]{3,2,1,0:T(8,128)(2,1)S(1)} copy(bf16[1,128,8,256]{3,1,2,0:T(8,128)(2,1)} %bitcast.11) | data formatting | bytes 1048576 | tf_op jit(solution)/shard_map/transpose | solution.py:369
  2.0 3.1 %collective-permute-start = (bf16[1,512,256]{2,1,0:T(8,128)(2,1)S(1)}, bf16[1,512,256]{2,1,0:T(8,128)(2,1)S(1)}, u32[]{:S(2)}, u32[]{:S(2)}) collective-permute-start(bf16[1,512,256]{2,1,0:T(8,128)(2,1)S(1)} %get-tuple-element.66), channel_id=1, source_target_pairs={{0,2},{1,3},{2,0},{3,1},{4,6},{5,7},{6,4},{7,5},{8,10},{9,11},{10,... | collective-permute-start | bytes 786440 | tf_op jit(solution)/shard_map/ppermute | solution.py:358
  5.1 2.6 %collective-permute-start.1 = (bf16[1,512,256]{2,1,0:T(8,128)(2,1)S(1)}, bf16[1,512,256]{2,1,0:T(8,128)(2,1)S(1)}, u32[]{:S(2)}, u32[]{:S(2)}) collective-permute-start(bf16[1,512,256]{2,1,0:T(8,128)(2,1)S(1)} %get-tuple-element.66), channel_id=1, source_target_pairs={{0,4},{1,5},{2,6},{3,7},{4,0},{5,1},{6,2},{7,3},{8,12},{9,13},{10,... | collective-permute-start | bytes 786440 | tf_op jit(solution)/shard_map/ppermute | solution.py:358
  7.7 19.2 %front.1 = (bf16[128,96,256]{2,1,0:T(8,128)(2,1)}, f32[4,512,256]{2,1,0:T(8,128)S(1)}, bf16[4,520,256]{2,1,0:T(8,128)(2,1)S(1)}, f32[4,8,128]{2,1,0:T(8,128)S(1)}) custom-call(s32[96]{0:T(128)} %bitcast.15, s32[96]{0:T(128)} %orient_ref.1, s32[96]{0:T(128)} %bin_ref.1, bf16[96,256,256]{2,1,0:T(8,128)(2,1)} %img_ref.1, ...), custom_call_target="tpu_custom_call" | custom-call | flops 12884901888 | bytes 25165824 | tf_op jit(solution)/shard_map/front/pallas_call | solution.py:108
  26.9 0.0 collective-permute-done
  26.9 0.0 collective-permute-done.1
  26.9 0.1 collective-permute-start.3
  27.0 0.1 pad_maximum_fusion.refs_0_
  27.2 0.6 collective-permute-start.7
  27.8 0.1 fusion
  27.9 1.8 %collective-permute-start.8 = (bf16[3,256,256]{2,1,0:T(8,128)(2,1)S(1)}, bf16[3,256,256]{2,1,0:T(8,128)(2,1)S(1)}, u32[]{:S(2)}, u32[]{:S(2)}) collective-permute-start(bf16[3,256,256]{2,1,0:T(8,128)(2,1)S(1)} %get-tuple-element.64), channel_id=1, source_target_pairs={{0,8},{8,0},{16,24},{24,16},{1,9},{9,1},{17,25},{25,17},{2,10},{10... | collective-permute-start | bytes 1179656 | tf_op jit(solution)/shard_map/ppermute | solution.py:358
  29.6 1.5 %collective-permute-start.9 = (bf16[3,256,256]{2,1,0:T(8,128)(2,1)S(1)}, bf16[3,256,256]{2,1,0:T(8,128)(2,1)S(1)}, u32[]{:S(2)}, u32[]{:S(2)}) collective-permute-start(bf16[3,256,256]{2,1,0:T(8,128)(2,1)S(1)} %get-tuple-element.63), channel_id=1, source_target_pairs={{0,16},{8,24},{16,0},{24,8},{1,17},{9,25},{17,1},{25,9},{2,18},{10... | collective-permute-start | bytes 1179656 | tf_op jit(solution)/shard_map/ppermute | solution.py:358
  31.1 0.0 collective-permute-done.3.got_ref
  31.1 0.3 chip_sum.1
  31.5 0.6 collective-permute-start.4
  32.1 1.2 %collective-permute-start.5 = (bf16[4,136,256]{2,1,0:T(8,128)(2,1)S(1)}, bf16[4,136,256]{2,1,0:T(8,128)(2,1)S(1)}, u32[]{:S(2)}, u32[]{:S(2)}) collective-permute-start(bf16[4,136,256]{2,1,0:T(8,128)(2,1)S(1)} %get-tuple-element.40), channel_id=1, source_target_pairs={{0,16},{8,24},{16,0},{24,8},{1,17},{9,25},{17,1},{25,9},{2,18},{10... | collective-permute-start | bytes 835592 | tf_op jit(solution)/shard_map/ppermute | solution.py:358
  33.3 1.7 %collective-permute-start.6 = (bf16[4,136,256]{2,1,0:T(8,128)(2,1)S(1)}, bf16[4,136,256]{2,1,0:T(8,128)(2,1)S(1)}, u32[]{:S(2)}, u32[]{:S(2)}) collective-permute-start(bf16[4,136,256]{2,1,0:T(8,128)(2,1)S(1)} %get-tuple-element.41), channel_id=1, source_target_pairs={{0,24},{8,16},{16,8},{24,0},{1,25},{9,17},{17,9},{25,1},{2,26},{10... | collective-permute-start | bytes 835592 | tf_op jit(solution)/shard_map/ppermute | solution.py:358
  35.0 3.1 %score.2.sum_ref = f32[2,96,128]{2,1,0:T(8,128)S(1)} custom-call(s32[1]{0:T(128)} %bitcast.3.first_ref, f32[2,96,128]{2,1,0:T(8,128)S(1)} %broadcast_in_dim.16.sum_ref, bf16[128,96,256]{2,1,0:T(8,128)(2,1)} %get-tuple-element.42.w_ref, bf16[4,512,256]{2,1,0:T(8,128)(2,1)} %copy-done.3, bf16[4,512,256]{2,1,0:T(8,128)(2,1)} %copy-done.5), custom_call_target="tpu_custom_call" | custom-call | tf_op jit(solution)/shard_map/score/pallas_call | solution.py:203
  38.1 1.8 %collective-permute-done.8 = bf16[3,256,256]{2,1,0:T(8,128)(2,1)S(1)} collective-permute-done((bf16[3,256,256]{2,1,0:T(8,128)(2,1)S(1)}, bf16[3,256,256]{2,1,0:T(8,128)(2,1)S(1)}, u32[]{:S(2)}, u32[]{:S(2)}) %collective-permute-start.8) | collective-permute-done | bytes 393248 | tf_op jit(solution)/shard_map/ppermute | solution.py:358
  39.9 1.7 %collective-permute-done.9 = bf16[3,256,256]{2,1,0:T(8,128)(2,1)S(1)} collective-permute-done((bf16[3,256,256]{2,1,0:T(8,128)(2,1)S(1)}, bf16[3,256,256]{2,1,0:T(8,128)(2,1)S(1)}, u32[]{:S(2)}, u32[]{:S(2)}) %collective-permute-start.9) | collective-permute-done | bytes 393248 | tf_op jit(solution)/shard_map/ppermute | solution.py:358
  41.6 4.2 %collective-permute-done.4.refs_0_ = bf16[4,136,256]{2,1,0:T(8,128)(2,1)S(1)} collective-permute-done((bf16[4,136,256]{2,1,0:T(8,128)(2,1)S(1)}, bf16[4,136,256]{2,1,0:T(8,128)(2,1)S(1)}, u32[]{:S(2)}, u32[]{:S(2)}) %collective-permute-start.4) | collective-permute-done | bytes 278560 | tf_op jit(solution)/shard_map/ppermute | solution.py:358
  45.9 6.4 %collective-permute-done.5.refs_1_ = bf16[4,136,256]{2,1,0:T(8,128)(2,1)S(1)} collective-permute-done((bf16[4,136,256]{2,1,0:T(8,128)(2,1)S(1)}, bf16[4,136,256]{2,1,0:T(8,128)(2,1)S(1)}, u32[]{:S(2)}, u32[]{:S(2)}) %collective-permute-start.5) | collective-permute-done | bytes 278560 | tf_op jit(solution)/shard_map/ppermute | solution.py:358
  52.3 0.1 maximum_maximum_fusion.refs_0_
  52.4 0.1 collective-permute-start.13
  52.5 0.2 plane_sum.1
  52.7 4.1 %collective-permute-start.10 = (bf16[136,256]{1,0:T(8,128)(2,1)S(1)}, bf16[136,256]{1,0:T(8,128)(2,1)S(1)}, u32[]{:S(2)}, u32[]{:S(2)}) collective-permute-start(bf16[136,256]{1,0:T(8,128)(2,1)S(1)} %get-tuple-element.49), channel_id=1, source_target_pairs={{0,2},{1,3},{2,0},{3,1},{4,6},{5,7},{6,4},{7,5},{8,10},{9,11},{10,... | collective-permute-start | bytes 208904 | tf_op jit(solution)/shard_map/ppermute | solution.py:358
  56.8 1.1 %collective-permute-start.11 = (bf16[136,256]{1,0:T(8,128)(2,1)S(1)}, bf16[136,256]{1,0:T(8,128)(2,1)S(1)}, u32[]{:S(2)}, u32[]{:S(2)}) collective-permute-start(bf16[136,256]{1,0:T(8,128)(2,1)S(1)} %get-tuple-element.50), channel_id=1, source_target_pairs={{0,4},{1,5},{2,6},{3,7},{4,0},{5,1},{6,2},{7,3},{8,12},{9,13},{10,... | collective-permute-start | bytes 208904 | tf_op jit(solution)/shard_map/ppermute | solution.py:358
  57.9 1.4 %collective-permute-start.12 = (bf16[136,256]{1,0:T(8,128)(2,1)S(1)}, bf16[136,256]{1,0:T(8,128)(2,1)S(1)}, u32[]{:S(2)}, u32[]{:S(2)}) collective-permute-start(bf16[136,256]{1,0:T(8,128)(2,1)S(1)} %get-tuple-element.51), channel_id=1, source_target_pairs={{0,6},{1,7},{2,4},{3,5},{4,2},{5,3},{6,0},{7,1},{8,14},{9,15},{10,... | collective-permute-start | bytes 208904 | tf_op jit(solution)/shard_map/ppermute | solution.py:358
  59.3 1.1 %copy-done.6 = bf16[4,512,256]{2,1,0:T(8,128)(2,1)} copy-done((bf16[4,512,256]{2,1,0:T(8,128)(2,1)}, bf16[4,512,256]{2,1,0:T(8,128)(2,1)S(1)}, u32[]{:S(2)}) %copy-start.6) | copy-done | bytes 1048600
  60.3 3.8 %score.3 = f32[1,96]{1,0:T(1,128)} custom-call(s32[1]{0:T(128)} %bitcast.4.first_ref, f32[2,96,128]{2,1,0:T(8,128)S(1)} %score.2.sum_ref, bf16[128,96,256]{2,1,0:T(8,128)(2,1)} %get-tuple-element.42.w_ref, bf16[4,512,256]{2,1,0:T(8,128)(2,1)} %copy-done.4, bf16[4,512,256]{2,1,0:T(8,128)(2,1)} %copy-done.6), custom_call_target="tpu_custom_call" | custom-call | tf_op jit(solution)/shard_map/score/pallas_call | solution.py:203
  64.1 1.2 %collective-permute-done.11.refs_1_ = bf16[136,256]{1,0:T(8,128)(2,1)S(1)} collective-permute-done((bf16[136,256]{1,0:T(8,128)(2,1)S(1)}, bf16[136,256]{1,0:T(8,128)(2,1)S(1)}, u32[]{:S(2)}, u32[]{:S(2)}) %collective-permute-start.11) | collective-permute-done | bytes 69664 | tf_op jit(solution)/shard_map/ppermute | solution.py:358
  65.4 2.6 %final_sum.1 = (f32[128,256]{1,0:T(8,128)}, f32[128,256]{1,0:T(8,128)}) custom-call(f32[16,128,256]{2,1,0:T(8,128)S(1)} %copy-done, s32[8,128]{1,0:T(8,128)S(1)} %copy-done.1, f32[8,128]{1,0:T(8,128)S(1)} %copy-done.2, f32[128,256]{1,0:T(8,128)S(1)} %get-tuple-element.56.own_ref, f32[8,128]{1,0:T(8,128)S(1)} %get-tuple-element.57.count_ref, ...), custom_call_target="tpu_custom_call" | custom-call | tf_op jit(solution)/shard_map/final_sum/pallas_call | solution.py:342
  (25 shorter events, 0.2 us)
Async XLA Ops:
  2.0 24.9 %collective-permute-start = (bf16[1,512,256]{2,1,0:T(8,128)(2,1)S(1)}, bf16[1,512,256]{2,1,0:T(8,128)(2,1)S(1)}, u32[]{:S(2)}, u32[]{:S(2)}) collective-permute-start(bf16[1,512,256]{2,1,0:T(8,128)(2,1)S(1)} %get-tuple-element.66), channel_id=1, source_target_pairs={{0,2},{1,3},{2,0},{3,1},{4,6},{5,7},{6,4},{7,5},{8,10},{9,11},{10,... | collective-permute-start | bytes 786440 | tf_op jit(solution)/shard_map/ppermute | solution.py:358
  5.1 21.8 %collective-permute-start.1 = (bf16[1,512,256]{2,1,0:T(8,128)(2,1)S(1)}, bf16[1,512,256]{2,1,0:T(8,128)(2,1)S(1)}, u32[]{:S(2)}, u32[]{:S(2)}) collective-permute-start(bf16[1,512,256]{2,1,0:T(8,128)(2,1)S(1)} %get-tuple-element.66), channel_id=1, source_target_pairs={{0,4},{1,5},{2,6},{3,7},{4,0},{5,1},{6,2},{7,3},{8,12},{9,13},{10,... | collective-permute-start | bytes 786440 | tf_op jit(solution)/shard_map/ppermute | solution.py:358
  7.7 19.2 %collective-permute-start.2 = (bf16[1,512,256]{2,1,0:T(8,128)(2,1)S(1)}, bf16[1,512,256]{2,1,0:T(8,128)(2,1)S(1)}, u32[]{:S(2)}, u32[]{:S(2)}) collective-permute-start(bf16[1,512,256]{2,1,0:T(8,128)(2,1)S(1)} %get-tuple-element.66), channel_id=1, source_target_pairs={{0,6},{1,7},{2,4},{3,5},{4,2},{5,3},{6,0},{7,1},{8,14},{9,15},{10,... | collective-permute-start | bytes 786440 | tf_op jit(solution)/shard_map/ppermute | solution.py:358
  26.9 4.2 %collective-permute-start.3 = (bf16[4,520,256]{2,1,0:T(8,128)(2,1)S(1)}, bf16[4,520,256]{2,1,0:T(8,128)(2,1)S(1)}, u32[]{:S(2)}, u32[]{:S(2)}) collective-permute-start(bf16[4,520,256]{2,1,0:T(8,128)(2,1)S(1)} %get-tuple-element.36), channel_id=1, source_target_pairs={{0,1},{1,0},{2,3},{3,2},{4,5},{5,4},{6,7},{7,6},{8,9},{9,8},{10,11... | collective-permute-start | bytes 3194888 | tf_op jit(solution)/shard_map/ppermute | solution.py:358
  27.2 4.3 %copy-start.3 = (bf16[4,512,256]{2,1,0:T(8,128)(2,1)}, bf16[4,512,256]{2,1,0:T(8,128)(2,1)S(1)}, u32[]{:S(2)}) copy-start(bf16[4,512,256]{2,1,0:T(8,128)(2,1)S(1)} %pad_maximum_fusion.refs_0_) | copy-start | bytes 3145732
  27.2 6.1 %collective-permute-start.7 = (bf16[4,512,256]{2,1,0:T(8,128)(2,1)S(1)}, bf16[4,512,256]{2,1,0:T(8,128)(2,1)S(1)}, u32[]{:S(2)}, u32[]{:S(2)}) collective-permute-start(bf16[4,512,256]{2,1,0:T(8,128)(2,1)S(1)} %pad_maximum_fusion.refs_0_), channel_id=1, source_target_pairs={{0,1},{1,0},{2,3},{3,2},{4,5},{5,4},{6,7},{7,6},{8,9},{9,8},{10,11... | collective-permute-start | bytes 3145736 | tf_op jit(solution)/shard_map/ppermute | solution.py:358
  27.9 12.0 %collective-permute-start.8 = (bf16[3,256,256]{2,1,0:T(8,128)(2,1)S(1)}, bf16[3,256,256]{2,1,0:T(8,128)(2,1)S(1)}, u32[]{:S(2)}, u32[]{:S(2)}) collective-permute-start(bf16[3,256,256]{2,1,0:T(8,128)(2,1)S(1)} %get-tuple-element.64), channel_id=1, source_target_pairs={{0,8},{8,0},{16,24},{24,16},{1,9},{9,1},{17,25},{25,17},{2,10},{10... | collective-permute-start | bytes 1179656 | tf_op jit(solution)/shard_map/ppermute | solution.py:358
  29.6 12.0 %collective-permute-start.9 = (bf16[3,256,256]{2,1,0:T(8,128)(2,1)S(1)}, bf16[3,256,256]{2,1,0:T(8,128)(2,1)S(1)}, u32[]{:S(2)}, u32[]{:S(2)}) collective-permute-start(bf16[3,256,256]{2,1,0:T(8,128)(2,1)S(1)} %get-tuple-element.63), channel_id=1, source_target_pairs={{0,16},{8,24},{16,0},{24,8},{1,17},{9,25},{17,1},{25,9},{2,18},{10... | collective-permute-start | bytes 1179656 | tf_op jit(solution)/shard_map/ppermute | solution.py:358
  31.5 14.4 %collective-permute-start.4 = (bf16[4,136,256]{2,1,0:T(8,128)(2,1)S(1)}, bf16[4,136,256]{2,1,0:T(8,128)(2,1)S(1)}, u32[]{:S(2)}, u32[]{:S(2)}) collective-permute-start(bf16[4,136,256]{2,1,0:T(8,128)(2,1)S(1)} %get-tuple-element.39), channel_id=1, source_target_pairs={{0,8},{8,0},{16,24},{24,16},{1,9},{9,1},{17,25},{25,17},{2,10},{10... | collective-permute-start | bytes 835592 | tf_op jit(solution)/shard_map/ppermute | solution.py:358
  32.1 20.3 %collective-permute-start.5 = (bf16[4,136,256]{2,1,0:T(8,128)(2,1)S(1)}, bf16[4,136,256]{2,1,0:T(8,128)(2,1)S(1)}, u32[]{:S(2)}, u32[]{:S(2)}) collective-permute-start(bf16[4,136,256]{2,1,0:T(8,128)(2,1)S(1)} %get-tuple-element.40), channel_id=1, source_target_pairs={{0,16},{8,24},{16,0},{24,8},{1,17},{9,25},{17,1},{25,9},{2,18},{10... | collective-permute-start | bytes 835592 | tf_op jit(solution)/shard_map/ppermute | solution.py:358
  33.3 1.7 %copy-start.5 = (bf16[4,512,256]{2,1,0:T(8,128)(2,1)}, bf16[4,512,256]{2,1,0:T(8,128)(2,1)S(1)}, u32[]{:S(2)}) copy-start(bf16[4,512,256]{2,1,0:T(8,128)(2,1)S(1)} %collective-permute-done.7.refs_1_) | copy-start | bytes 3145732
  33.3 19.0 %collective-permute-start.6 = (bf16[4,136,256]{2,1,0:T(8,128)(2,1)S(1)}, bf16[4,136,256]{2,1,0:T(8,128)(2,1)S(1)}, u32[]{:S(2)}, u32[]{:S(2)}) collective-permute-start(bf16[4,136,256]{2,1,0:T(8,128)(2,1)S(1)} %get-tuple-element.41), channel_id=1, source_target_pairs={{0,24},{8,16},{16,8},{24,0},{1,25},{9,17},{17,9},{25,1},{2,26},{10... | collective-permute-start | bytes 835592 | tf_op jit(solution)/shard_map/ppermute | solution.py:358
  52.4 6.8 %copy-start.4 = (bf16[4,512,256]{2,1,0:T(8,128)(2,1)}, bf16[4,512,256]{2,1,0:T(8,128)(2,1)S(1)}, u32[]{:S(2)}) copy-start(bf16[4,512,256]{2,1,0:T(8,128)(2,1)S(1)} %maximum_maximum_fusion.refs_0_) | copy-start | bytes 3145732
  52.4 6.8 %collective-permute-start.13 = (bf16[4,512,256]{2,1,0:T(8,128)(2,1)S(1)}, bf16[4,512,256]{2,1,0:T(8,128)(2,1)S(1)}, u32[]{:S(2)}, u32[]{:S(2)}) collective-permute-start(bf16[4,512,256]{2,1,0:T(8,128)(2,1)S(1)} %maximum_maximum_fusion.refs_0_), channel_id=1, source_target_pairs={{0,1},{1,0},{2,3},{3,2},{4,5},{5,4},{6,7},{7,6},{8,9},{9,8},{10,11... | collective-permute-start | bytes 3145736 | tf_op jit(solution)/shard_map/ppermute | solution.py:358
  52.7 11.5 %collective-permute-start.10 = (bf16[136,256]{1,0:T(8,128)(2,1)S(1)}, bf16[136,256]{1,0:T(8,128)(2,1)S(1)}, u32[]{:S(2)}, u32[]{:S(2)}) collective-permute-start(bf16[136,256]{1,0:T(8,128)(2,1)S(1)} %get-tuple-element.49), channel_id=1, source_target_pairs={{0,2},{1,3},{2,0},{3,1},{4,6},{5,7},{6,4},{7,5},{8,10},{9,11},{10,... | collective-permute-start | bytes 208904 | tf_op jit(solution)/shard_map/ppermute | solution.py:358
  56.8 8.6 %collective-permute-start.11 = (bf16[136,256]{1,0:T(8,128)(2,1)S(1)}, bf16[136,256]{1,0:T(8,128)(2,1)S(1)}, u32[]{:S(2)}, u32[]{:S(2)}) collective-permute-start(bf16[136,256]{1,0:T(8,128)(2,1)S(1)} %get-tuple-element.50), channel_id=1, source_target_pairs={{0,4},{1,5},{2,6},{3,7},{4,0},{5,1},{6,2},{7,3},{8,12},{9,13},{10,... | collective-permute-start | bytes 208904 | tf_op jit(solution)/shard_map/ppermute | solution.py:358
  57.9 7.5 %collective-permute-start.12 = (bf16[136,256]{1,0:T(8,128)(2,1)S(1)}, bf16[136,256]{1,0:T(8,128)(2,1)S(1)}, u32[]{:S(2)}, u32[]{:S(2)}) collective-permute-start(bf16[136,256]{1,0:T(8,128)(2,1)S(1)} %get-tuple-element.51), channel_id=1, source_target_pairs={{0,6},{1,7},{2,4},{3,5},{4,2},{5,3},{6,0},{7,1},{8,14},{9,15},{10,... | collective-permute-start | bytes 208904 | tf_op jit(solution)/shard_map/ppermute | solution.py:358
  59.2 1.1 %copy-start.6 = (bf16[4,512,256]{2,1,0:T(8,128)(2,1)}, bf16[4,512,256]{2,1,0:T(8,128)(2,1)S(1)}, u32[]{:S(2)}) copy-start(bf16[4,512,256]{2,1,0:T(8,128)(2,1)S(1)} %collective-permute-done.13.refs_1_) | copy-start | bytes 3145732
  60.3 5.1 %copy-start = (f32[16,128,256]{2,1,0:T(8,128)S(1)}, f32[16,128,256]{2,1,0:T(8,128)}, u32[]{:S(2)}) copy-start(f32[16,128,256]{2,1,0:T(8,128)} %ctf_ref.3) | copy-start | bytes 6291460
  60.3 5.1 %copy-start.1 = (s32[8,128]{1,0:T(8,128)S(1)}, s32[8,128]{1,0:T(8,128)}, u32[]{:S(2)}) copy-start(s32[8,128]{1,0:T(8,128)} %slot_ref.3) | copy-start | bytes 12292
  60.3 5.1 %copy-start.2 = (f32[8,128]{1,0:T(8,128)S(1)}, f32[8,128]{1,0:T(8,128)}, u32[]{:S(2)}) copy-start(f32[8,128]{1,0:T(8,128)} %wt_ref.3) | copy-start | bytes 12292

commit v4 on v3

--- a/solution.py
+++ b/solution.py
@@ -319,7 +319,7 @@
         for b in range(1, bin_count):
             value = value + squares[b] * count[o : o + 1, b : b + 1]
         value = value * wt_cols[:, o : o + 1]
-        for part in range(3):
+        for part in range(2):
             piece = value.astype(jnp.bfloat16)
             scr[pl.ds(o * rows, rows), pl.ds(part * pixels, pixels)] = piece
             value = value - piece.astype(jnp.float32)
@@ -332,7 +332,7 @@
         axis=1,
     )
     slab = jnp.dot(hot, scr[...], preferred_element_type=jnp.float32)
-    weight_ref[...] = (slab[:, 2 * pixels :] + slab[:, pixels : 2 * pixels]) + slab[:, :pixels]
+    weight_ref[...] = slab[:, pixels:] + slab[:, :pixels]
 
 
 def final_sum(ctf_table, slice_slots, slot_weight, own, count, gots):
@@ -346,7 +346,7 @@
         out_shape=[jax.ShapeDtypeStruct(own.shape, jnp.float32)] * 2,
         scratch_shapes=[
             pltpu.VMEM((bin_count, rows, pixels), jnp.float32),
-            pltpu.VMEM((orients * rows, 3 * pixels), jnp.bfloat16),
+            pltpu.VMEM((orients * rows, 2 * pixels), jnp.bfloat16),
         ],
         compiler_params=pltpu.CompilerParams(vmem_limit_bytes=12 * 2**20),
         name="final_sum",
@@ -366,11 +366,14 @@
     rows, pixels = ctf_table.shape[1], images.shape[2]
     orients = slot_weight.shape[0]
     near_rows = rows * 1 // 2
-    own_panel = jnp.transpose(projections, (0, 2, 1, 3)).reshape(1, -1, pixels)
     cut = near_rows * orients
     my_img = lax.axis_index("img")
     parity = (my_img ^ (my_img >> 1)) & 1
-    half = lambda p: lax.dynamic_slice_in_dim(own_panel, p * cut, cut, axis=1)
+
+    def half(p):
+        taken = lax.dynamic_slice_in_dim(projections, p * near_rows, near_rows, axis=2)
+        return jnp.transpose(taken, (0, 2, 1, 3)).reshape(1, cut, pixels)
+
     near = [swap(half(parity), "cls", 2 * m) for m in range(1, groups)]
     w2, keep, send, count = front(
         images,

time: 68.3 us -> 67.9 us (level)
    transpose x1 -> x3, local copies, waits for them, and re-layouts: 1.33 us -> 1.38 us  [half(): return jnp.transpose(taken, (0, 2, 1, 3)).reshape(1, cut, pixels)]
  transfers between devices with their start and end apart: 14 -> 14, of which waited for: 5 -> 5; matrix products, arithmetic and copies ran while one was open for 0% -> 1% of each run, Pallas kernels for 39% -> 39%
where the time goes in v4:
time: 67.9 us; the launch traced here: 67.6 us
  Pallas kernels  28.9 us (43%)
  starting transfers between devices  19.8 us (29%)
  waiting for transfers between devices  15.3 us (23%)
  local copies, waits for them, and re-layouts  2.59 us (4%)
  between operations  0.81 us (1%)
    ppermute x14, starting transfers between devices, swap(): return lax.ppermute(value, axis, [(i, i ^ mask) for i in range(size)])  19.8 us
    pallas_call x1, Pallas kernels, front(): pl.pallas_call(functools.partial(front_kernel, blocks), grid_spec=pltpu.P...  19.2 us
    ppermute x14, waiting for transfers between devices, swap(): return lax.ppermute(value, axis, [(i, i ^ mask) for i in range(size)])  15.3 us
    pallas_call x2, Pallas kernels, score(): pl.pallas_call(functools.partial(score_kernel, orients, last), grid_spec=...  6.89 us
    pallas_call x1, Pallas kernels, final_sum(): pl.pallas_call(final_kernel, in_specs=[vmem] * (5 + len(gots)), out_specs...  2.35 us
    transpose x3, local copies, waits for them, and re-layouts, half(): return jnp.transpose(taken, (0, 2, 1, 3)).reshape(1, cut, pixels)  1.38 us
  transfers between devices with their start and end apart: 14, of which 5 were waited for; matrix products, arithmetic and copies ran while one was open for 1% of the time, Pallas kernels for 39%

profile of v4, /device:TPU:0, one launch (start us, length us, event | category | flops | bytes accessed | tf_op | source)
XLA Modules:
  0.0 67.6 jit_solution(12809684130665326883)
XLA Ops:
  0.6 1.1 %dynamic-slice_bitcast_fusion = (bf16[1,64,8,256]{3,1,2,0:T(8,128)(2,1)S(1)}, bf16[1,64,8,256]{3,1,2,0:T(8,128)(2,1)S(1)}) fusion(bf16[1,8,128,256]{3,2,1,0:T(8,128)(2,1)} %param.12, s32[]{:T(128)S(6)} %select_n.10, s32[]{:T(128)S(6)} %select_n.4), kind=kLoop, calls=%fused_computation.4 | loop fusion | bytes 1048584 | tf_op jit(solution)/shard_map/transpose | solution.py:375
  1.7 0.2 copy.17
  1.9 3.1 %collective-permute-start = (bf16[1,512,256]{2,1,0:T(8,128)(2,1)S(1)}, bf16[1,512,256]{2,1,0:T(8,128)(2,1)S(1)}, u32[]{:S(2)}, u32[]{:S(2)}) collective-permute-start(bf16[1,512,256]{2,1,0:T(8,128)(2,1)S(1)} %bitcast.16), channel_id=1, source_target_pairs={{0,2},{1,3},{2,0},{3,1},{4,6},{5,7},{6,4},{7,5},{8,10},{9,11},{10,... | collective-permute-start | bytes 786440 | tf_op jit(solution)/shard_map/ppermute | solution.py:358
  5.0 2.6 %collective-permute-start.1 = (bf16[1,512,256]{2,1,0:T(8,128)(2,1)S(1)}, bf16[1,512,256]{2,1,0:T(8,128)(2,1)S(1)}, u32[]{:S(2)}, u32[]{:S(2)}) collective-permute-start(bf16[1,512,256]{2,1,0:T(8,128)(2,1)S(1)} %bitcast.17), channel_id=1, source_target_pairs={{0,4},{1,5},{2,6},{3,7},{4,0},{5,1},{6,2},{7,3},{8,12},{9,13},{10,... | collective-permute-start | bytes 786440 | tf_op jit(solution)/shard_map/ppermute | solution.py:358
  7.6 19.2 %front.1 = (bf16[128,96,256]{2,1,0:T(8,128)(2,1)}, f32[4,512,256]{2,1,0:T(8,128)S(1)}, bf16[4,520,256]{2,1,0:T(8,128)(2,1)S(1)}, f32[4,8,128]{2,1,0:T(8,128)S(1)}) custom-call(s32[96]{0:T(128)} %bitcast.24, s32[96]{0:T(128)} %orient_ref.1, s32[96]{0:T(128)} %bin_ref.1, bf16[96,256,256]{2,1,0:T(8,128)(2,1)} %img_ref.1, ...), custom_call_target="tpu_custom_call" | custom-call | flops 12884901888 | bytes 25165824 | tf_op jit(solution)/shard_map/front/pallas_call | solution.py:108
  26.8 0.0 collective-permute-done
  26.8 0.1 collective-permute-start.3
  26.9 0.1 pad_maximum_fusion.refs_0_
  27.0 0.6 collective-permute-start.7
  27.7 0.1 fusion
  27.7 1.7 %collective-permute-start.8 = (bf16[3,256,256]{2,1,0:T(8,128)(2,1)S(1)}, bf16[3,256,256]{2,1,0:T(8,128)(2,1)S(1)}, u32[]{:S(2)}, u32[]{:S(2)}) collective-permute-start(bf16[3,256,256]{2,1,0:T(8,128)(2,1)S(1)} %get-tuple-element.64), channel_id=1, source_target_pairs={{0,8},{8,0},{16,24},{24,16},{1,9},{9,1},{17,25},{25,17},{2,10},{10... | collective-permute-start | bytes 1179656 | tf_op jit(solution)/shard_map/ppermute | solution.py:358
  29.5 1.5 %collective-permute-start.9 = (bf16[3,256,256]{2,1,0:T(8,128)(2,1)S(1)}, bf16[3,256,256]{2,1,0:T(8,128)(2,1)S(1)}, u32[]{:S(2)}, u32[]{:S(2)}) collective-permute-start(bf16[3,256,256]{2,1,0:T(8,128)(2,1)S(1)} %get-tuple-element.63), channel_id=1, source_target_pairs={{0,16},{8,24},{16,0},{24,8},{1,17},{9,25},{17,1},{25,9},{2,18},{10... | collective-permute-start | bytes 1179656 | tf_op jit(solution)/shard_map/ppermute | solution.py:358
  31.0 0.3 chip_sum.1
  31.3 0.6 collective-permute-start.4
  31.9 1.2 %collective-permute-start.5 = (bf16[4,136,256]{2,1,0:T(8,128)(2,1)S(1)}, bf16[4,136,256]{2,1,0:T(8,128)(2,1)S(1)}, u32[]{:S(2)}, u32[]{:S(2)}) collective-permute-start(bf16[4,136,256]{2,1,0:T(8,128)(2,1)S(1)} %get-tuple-element.40), channel_id=1, source_target_pairs={{0,16},{8,24},{16,0},{24,8},{1,17},{9,25},{17,1},{25,9},{2,18},{10... | collective-permute-start | bytes 835592 | tf_op jit(solution)/shard_map/ppermute | solution.py:358
  33.1 1.7 %collective-permute-start.6 = (bf16[4,136,256]{2,1,0:T(8,128)(2,1)S(1)}, bf16[4,136,256]{2,1,0:T(8,128)(2,1)S(1)}, u32[]{:S(2)}, u32[]{:S(2)}) collective-permute-start(bf16[4,136,256]{2,1,0:T(8,128)(2,1)S(1)} %get-tuple-element.41), channel_id=1, source_target_pairs={{0,24},{8,16},{16,8},{24,0},{1,25},{9,17},{17,9},{25,1},{2,26},{10... | collective-permute-start | bytes 835592 | tf_op jit(solution)/shard_map/ppermute | solution.py:358
  34.9 0.1 copy.16
  35.0 3.1 %score.2.sum_ref = f32[2,96,128]{2,1,0:T(8,128)S(1)} custom-call(s32[1]{0:T(128)} %bitcast.3.first_ref, f32[2,96,128]{2,1,0:T(8,128)S(1)} %broadcast_in_dim.16.sum_ref, bf16[128,96,256]{2,1,0:T(8,128)(2,1)} %get-tuple-element.42.w_ref, bf16[4,512,256]{2,1,0:T(8,128)(2,1)} %copy-done.3, bf16[4,512,256]{2,1,0:T(8,128)(2,1)} %copy-done.5), custom_call_target="tpu_custom_call" | custom-call | tf_op jit(solution)/shard_map/score/pallas_call | solution.py:203
  38.1 1.6 %collective-permute-done.8 = bf16[3,256,256]{2,1,0:T(8,128)(2,1)S(1)} collective-permute-done((bf16[3,256,256]{2,1,0:T(8,128)(2,1)S(1)}, bf16[3,256,256]{2,1,0:T(8,128)(2,1)S(1)}, u32[]{:S(2)}, u32[]{:S(2)}) %collective-permute-start.8) | collective-permute-done | bytes 393248 | tf_op jit(solution)/shard_map/ppermute | solution.py:358
  39.8 1.7 %collective-permute-done.9 = bf16[3,256,256]{2,1,0:T(8,128)(2,1)S(1)} collective-permute-done((bf16[3,256,256]{2,1,0:T(8,128)(2,1)S(1)}, bf16[3,256,256]{2,1,0:T(8,128)(2,1)S(1)}, u32[]{:S(2)}, u32[]{:S(2)}) %collective-permute-start.9) | collective-permute-done | bytes 393248 | tf_op jit(solution)/shard_map/ppermute | solution.py:358
  41.5 4.2 %collective-permute-done.4.refs_0_ = bf16[4,136,256]{2,1,0:T(8,128)(2,1)S(1)} collective-permute-done((bf16[4,136,256]{2,1,0:T(8,128)(2,1)S(1)}, bf16[4,136,256]{2,1,0:T(8,128)(2,1)S(1)}, u32[]{:S(2)}, u32[]{:S(2)}) %collective-permute-start.4) | collective-permute-done | bytes 278560 | tf_op jit(solution)/shard_map/ppermute | solution.py:358
  45.7 6.4 %collective-permute-done.5.refs_1_ = bf16[4,136,256]{2,1,0:T(8,128)(2,1)S(1)} collective-permute-done((bf16[4,136,256]{2,1,0:T(8,128)(2,1)S(1)}, bf16[4,136,256]{2,1,0:T(8,128)(2,1)S(1)}, u32[]{:S(2)}, u32[]{:S(2)}) %collective-permute-start.5) | collective-permute-done | bytes 278560 | tf_op jit(solution)/shard_map/ppermute | solution.py:358
  52.2 0.1 maximum_maximum_fusion.refs_0_
  52.3 0.1 collective-permute-start.13
  52.3 0.2 plane_sum.1
  52.5 4.1 %collective-permute-start.10 = (bf16[136,256]{1,0:T(8,128)(2,1)S(1)}, bf16[136,256]{1,0:T(8,128)(2,1)S(1)}, u32[]{:S(2)}, u32[]{:S(2)}) collective-permute-start(bf16[136,256]{1,0:T(8,128)(2,1)S(1)} %get-tuple-element.49), channel_id=1, source_target_pairs={{0,2},{1,3},{2,0},{3,1},{4,6},{5,7},{6,4},{7,5},{8,10},{9,11},{10,... | collective-permute-start | bytes 208904 | tf_op jit(solution)/shard_map/ppermute | solution.py:358
  56.6 1.1 %collective-permute-start.11 = (bf16[136,256]{1,0:T(8,128)(2,1)S(1)}, bf16[136,256]{1,0:T(8,128)(2,1)S(1)}, u32[]{:S(2)}, u32[]{:S(2)}) collective-permute-start(bf16[136,256]{1,0:T(8,128)(2,1)S(1)} %get-tuple-element.50), channel_id=1, source_target_pairs={{0,4},{1,5},{2,6},{3,7},{4,0},{5,1},{6,2},{7,3},{8,12},{9,13},{10,... | collective-permute-start | bytes 208904 | tf_op jit(solution)/shard_map/ppermute | solution.py:358
  57.7 1.4 %collective-permute-start.12 = (bf16[136,256]{1,0:T(8,128)(2,1)S(1)}, bf16[136,256]{1,0:T(8,128)(2,1)S(1)}, u32[]{:S(2)}, u32[]{:S(2)}) collective-permute-start(bf16[136,256]{1,0:T(8,128)(2,1)S(1)} %get-tuple-element.51), channel_id=1, source_target_pairs={{0,6},{1,7},{2,4},{3,5},{4,2},{5,3},{6,0},{7,1},{8,14},{9,15},{10,... | collective-permute-start | bytes 208904 | tf_op jit(solution)/shard_map/ppermute | solution.py:358
  59.1 1.1 %copy-done.6 = bf16[4,512,256]{2,1,0:T(8,128)(2,1)} copy-done((bf16[4,512,256]{2,1,0:T(8,128)(2,1)}, bf16[4,512,256]{2,1,0:T(8,128)(2,1)S(1)}, u32[]{:S(2)}) %copy-start.6) | copy-done | bytes 1048600
  60.2 3.8 %score.3 = f32[1,96]{1,0:T(1,128)} custom-call(s32[1]{0:T(128)} %bitcast.4.first_ref, f32[2,96,128]{2,1,0:T(8,128)S(1)} %score.2.sum_ref, bf16[128,96,256]{2,1,0:T(8,128)(2,1)} %get-tuple-element.42.w_ref, bf16[4,512,256]{2,1,0:T(8,128)(2,1)} %copy-done.4, bf16[4,512,256]{2,1,0:T(8,128)(2,1)} %copy-done.6), custom_call_target="tpu_custom_call" | custom-call | tf_op jit(solution)/shard_map/score/pallas_call | solution.py:203
  64.0 1.2 %collective-permute-done.11.refs_1_ = bf16[136,256]{1,0:T(8,128)(2,1)S(1)} collective-permute-done((bf16[136,256]{1,0:T(8,128)(2,1)S(1)}, bf16[136,256]{1,0:T(8,128)(2,1)S(1)}, u32[]{:S(2)}, u32[]{:S(2)}) %collective-permute-start.11) | collective-permute-done | bytes 69664 | tf_op jit(solution)/shard_map/ppermute | solution.py:358
  65.2 2.4 %final_sum.1 = (f32[128,256]{1,0:T(8,128)}, f32[128,256]{1,0:T(8,128)}) custom-call(f32[16,128,256]{2,1,0:T(8,128)S(1)} %copy-done, s32[8,128]{1,0:T(8,128)S(1)} %copy-done.1, f32[8,128]{1,0:T(8,128)S(1)} %copy-done.2, f32[128,256]{1,0:T(8,128)S(1)} %get-tuple-element.56.own_ref, f32[8,128]{1,0:T(8,128)S(1)} %get-tuple-element.57.count_ref, ...), custom_call_target="tpu_custom_call" | custom-call | tf_op jit(solution)/shard_map/final_sum/pallas_call | solution.py:342
  (26 shorter events, 0.1 us)
Async XLA Ops:
  1.9 24.9 %collective-permute-start = (bf16[1,512,256]{2,1,0:T(8,128)(2,1)S(1)}, bf16[1,512,256]{2,1,0:T(8,128)(2,1)S(1)}, u32[]{:S(2)}, u32[]{:S(2)}) collective-permute-start(bf16[1,512,256]{2,1,0:T(8,128)(2,1)S(1)} %bitcast.16), channel_id=1, source_target_pairs={{0,2},{1,3},{2,0},{3,1},{4,6},{5,7},{6,4},{7,5},{8,10},{9,11},{10,... | collective-permute-start | bytes 786440 | tf_op jit(solution)/shard_map/ppermute | solution.py:358
  5.0 21.8 %collective-permute-start.1 = (bf16[1,512,256]{2,1,0:T(8,128)(2,1)S(1)}, bf16[1,512,256]{2,1,0:T(8,128)(2,1)S(1)}, u32[]{:S(2)}, u32[]{:S(2)}) collective-permute-start(bf16[1,512,256]{2,1,0:T(8,128)(2,1)S(1)} %bitcast.17), channel_id=1, source_target_pairs={{0,4},{1,5},{2,6},{3,7},{4,0},{5,1},{6,2},{7,3},{8,12},{9,13},{10,... | collective-permute-start | bytes 786440 | tf_op jit(solution)/shard_map/ppermute | solution.py:358
  7.6 19.2 %collective-permute-start.2 = (bf16[1,512,256]{2,1,0:T(8,128)(2,1)S(1)}, bf16[1,512,256]{2,1,0:T(8,128)(2,1)S(1)}, u32[]{:S(2)}, u32[]{:S(2)}) collective-permute-start(bf16[1,512,256]{2,1,0:T(8,128)(2,1)S(1)} %bitcast.18), channel_id=1, source_target_pairs={{0,6},{1,7},{2,4},{3,5},{4,2},{5,3},{6,0},{7,1},{8,14},{9,15},{10,... | collective-permute-start | bytes 786440 | tf_op jit(solution)/shard_map/ppermute | solution.py:358
  26.8 4.2 %collective-permute-start.3 = (bf16[4,520,256]{2,1,0:T(8,128)(2,1)S(1)}, bf16[4,520,256]{2,1,0:T(8,128)(2,1)S(1)}, u32[]{:S(2)}, u32[]{:S(2)}) collective-permute-start(bf16[4,520,256]{2,1,0:T(8,128)(2,1)S(1)} %get-tuple-element.36), channel_id=1, source_target_pairs={{0,1},{1,0},{2,3},{3,2},{4,5},{5,4},{6,7},{7,6},{8,9},{9,8},{10,11... | collective-permute-start | bytes 3194888 | tf_op jit(solution)/shard_map/ppermute | solution.py:358
  27.0 4.3 %copy-start.3 = (bf16[4,512,256]{2,1,0:T(8,128)(2,1)}, bf16[4,512,256]{2,1,0:T(8,128)(2,1)S(1)}, u32[]{:S(2)}) copy-start(bf16[4,512,256]{2,1,0:T(8,128)(2,1)S(1)} %pad_maximum_fusion.refs_0_) | copy-start | bytes 3145732
  27.0 6.1 %collective-permute-start.7 = (bf16[4,512,256]{2,1,0:T(8,128)(2,1)S(1)}, bf16[4,512,256]{2,1,0:T(8,128)(2,1)S(1)}, u32[]{:S(2)}, u32[]{:S(2)}) collective-permute-start(bf16[4,512,256]{2,1,0:T(8,128)(2,1)S(1)} %pad_maximum_fusion.refs_0_), channel_id=1, source_target_pairs={{0,1},{1,0},{2,3},{3,2},{4,5},{5,4},{6,7},{7,6},{8,9},{9,8},{10,11... | collective-permute-start | bytes 3145736 | tf_op jit(solution)/shard_map/ppermute | solution.py:358
  27.7 12.0 %collective-permute-start.8 = (bf16[3,256,256]{2,1,0:T(8,128)(2,1)S(1)}, bf16[3,256,256]{2,1,0:T(8,128)(2,1)S(1)}, u32[]{:S(2)}, u32[]{:S(2)}) collective-permute-start(bf16[3,256,256]{2,1,0:T(8,128)(2,1)S(1)} %get-tuple-element.64), channel_id=1, source_target_pairs={{0,8},{8,0},{16,24},{24,16},{1,9},{9,1},{17,25},{25,17},{2,10},{10... | collective-permute-start | bytes 1179656 | tf_op jit(solution)/shard_map/ppermute | solution.py:358
  29.5 12.0 %collective-permute-start.9 = (bf16[3,256,256]{2,1,0:T(8,128)(2,1)S(1)}, bf16[3,256,256]{2,1,0:T(8,128)(2,1)S(1)}, u32[]{:S(2)}, u32[]{:S(2)}) collective-permute-start(bf16[3,256,256]{2,1,0:T(8,128)(2,1)S(1)} %get-tuple-element.63), channel_id=1, source_target_pairs={{0,16},{8,24},{16,0},{24,8},{1,17},{9,25},{17,1},{25,9},{2,18},{10... | collective-permute-start | bytes 1179656 | tf_op jit(solution)/shard_map/ppermute | solution.py:358
  31.3 14.4 %collective-permute-start.4 = (bf16[4,136,256]{2,1,0:T(8,128)(2,1)S(1)}, bf16[4,136,256]{2,1,0:T(8,128)(2,1)S(1)}, u32[]{:S(2)}, u32[]{:S(2)}) collective-permute-start(bf16[4,136,256]{2,1,0:T(8,128)(2,1)S(1)} %get-tuple-element.39), channel_id=1, source_target_pairs={{0,8},{8,0},{16,24},{24,16},{1,9},{9,1},{17,25},{25,17},{2,10},{10... | collective-permute-start | bytes 835592 | tf_op jit(solution)/shard_map/ppermute | solution.py:358
  31.9 20.3 %collective-permute-start.5 = (bf16[4,136,256]{2,1,0:T(8,128)(2,1)S(1)}, bf16[4,136,256]{2,1,0:T(8,128)(2,1)S(1)}, u32[]{:S(2)}, u32[]{:S(2)}) collective-permute-start(bf16[4,136,256]{2,1,0:T(8,128)(2,1)S(1)} %get-tuple-element.40), channel_id=1, source_target_pairs={{0,16},{8,24},{16,0},{24,8},{1,17},{9,25},{17,1},{25,9},{2,18},{10... | collective-permute-start | bytes 835592 | tf_op jit(solution)/shard_map/ppermute | solution.py:358
  33.1 1.9 %copy-start.5 = (bf16[4,512,256]{2,1,0:T(8,128)(2,1)}, bf16[4,512,256]{2,1,0:T(8,128)(2,1)S(1)}, u32[]{:S(2)}) copy-start(bf16[4,512,256]{2,1,0:T(8,128)(2,1)S(1)} %collective-permute-done.7.refs_1_) | copy-start | bytes 3145732
  33.1 19.0 %collective-permute-start.6 = (bf16[4,136,256]{2,1,0:T(8,128)(2,1)S(1)}, bf16[4,136,256]{2,1,0:T(8,128)(2,1)S(1)}, u32[]{:S(2)}, u32[]{:S(2)}) collective-permute-start(bf16[4,136,256]{2,1,0:T(8,128)(2,1)S(1)} %get-tuple-element.41), channel_id=1, source_target_pairs={{0,24},{8,16},{16,8},{24,0},{1,25},{9,17},{17,9},{25,1},{2,26},{10... | collective-permute-start | bytes 835592 | tf_op jit(solution)/shard_map/ppermute | solution.py:358
  52.2 6.8 %copy-start.4 = (bf16[4,512,256]{2,1,0:T(8,128)(2,1)}, bf16[4,512,256]{2,1,0:T(8,128)(2,1)S(1)}, u32[]{:S(2)}) copy-start(bf16[4,512,256]{2,1,0:T(8,128)(2,1)S(1)} %maximum_maximum_fusion.refs_0_) | copy-start | bytes 3145732
  52.3 6.8 %collective-permute-start.13 = (bf16[4,512,256]{2,1,0:T(8,128)(2,1)S(1)}, bf16[4,512,256]{2,1,0:T(8,128)(2,1)S(1)}, u32[]{:S(2)}, u32[]{:S(2)}) collective-permute-start(bf16[4,512,256]{2,1,0:T(8,128)(2,1)S(1)} %maximum_maximum_fusion.refs_0_), channel_id=1, source_target_pairs={{0,1},{1,0},{2,3},{3,2},{4,5},{5,4},{6,7},{7,6},{8,9},{9,8},{10,11... | collective-permute-start | bytes 3145736 | tf_op jit(solution)/shard_map/ppermute | solution.py:358
  52.5 11.5 %collective-permute-start.10 = (bf16[136,256]{1,0:T(8,128)(2,1)S(1)}, bf16[136,256]{1,0:T(8,128)(2,1)S(1)}, u32[]{:S(2)}, u32[]{:S(2)}) collective-permute-start(bf16[136,256]{1,0:T(8,128)(2,1)S(1)} %get-tuple-element.49), channel_id=1, source_target_pairs={{0,2},{1,3},{2,0},{3,1},{4,6},{5,7},{6,4},{7,5},{8,10},{9,11},{10,... | collective-permute-start | bytes 208904 | tf_op jit(solution)/shard_map/ppermute | solution.py:358
  56.6 8.6 %collective-permute-start.11 = (bf16[136,256]{1,0:T(8,128)(2,1)S(1)}, bf16[136,256]{1,0:T(8,128)(2,1)S(1)}, u32[]{:S(2)}, u32[]{:S(2)}) collective-permute-start(bf16[136,256]{1,0:T(8,128)(2,1)S(1)} %get-tuple-element.50), channel_id=1, source_target_pairs={{0,4},{1,5},{2,6},{3,7},{4,0},{5,1},{6,2},{7,3},{8,12},{9,13},{10,... | collective-permute-start | bytes 208904 | tf_op jit(solution)/shard_map/ppermute | solution.py:358
  57.7 7.5 %collective-permute-start.12 = (bf16[136,256]{1,0:T(8,128)(2,1)S(1)}, bf16[136,256]{1,0:T(8,128)(2,1)S(1)}, u32[]{:S(2)}, u32[]{:S(2)}) collective-permute-start(bf16[136,256]{1,0:T(8,128)(2,1)S(1)} %get-tuple-element.51), channel_id=1, source_target_pairs={{0,6},{1,7},{2,4},{3,5},{4,2},{5,3},{6,0},{7,1},{8,14},{9,15},{10,... | collective-permute-start | bytes 208904 | tf_op jit(solution)/shard_map/ppermute | solution.py:358
  59.1 1.1 %copy-start.6 = (bf16[4,512,256]{2,1,0:T(8,128)(2,1)}, bf16[4,512,256]{2,1,0:T(8,128)(2,1)S(1)}, u32[]{:S(2)}) copy-start(bf16[4,512,256]{2,1,0:T(8,128)(2,1)S(1)} %collective-permute-done.13.refs_1_) | copy-start | bytes 3145732
  60.2 5.1 %copy-start = (f32[16,128,256]{2,1,0:T(8,128)S(1)}, f32[16,128,256]{2,1,0:T(8,128)}, u32[]{:S(2)}) copy-start(f32[16,128,256]{2,1,0:T(8,128)} %ctf_ref.3) | copy-start | bytes 6291460
  60.2 5.1 %copy-start.1 = (s32[8,128]{1,0:T(8,128)S(1)}, s32[8,128]{1,0:T(8,128)}, u32[]{:S(2)}) copy-start(s32[8,128]{1,0:T(8,128)} %slot_ref.3) | copy-start | bytes 12292
  60.2 5.1 %copy-start.2 = (f32[8,128]{1,0:T(8,128)S(1)}, f32[8,128]{1,0:T(8,128)}, u32[]{:S(2)}) copy-start(f32[8,128]{1,0:T(8,128)} %wt_ref.3) | copy-start | bytes 12292

commit v5 on v4

--- a/solution.py
+++ b/solution.py
@@ -391,7 +391,8 @@
     gots = [swap(part, "img", m + 1) for m, part in enumerate(parts)]
     near = jnp.concatenate([half(parity)] + near, axis=0)
     far = [swap(near[1:, : cut // 2], "img", 1), swap(near[1:, cut // 2 :], "img", 2)]
-    other = swap(near, "cls", 1)
+    _, later = lax.optimization_barrier((own_count, near))
+    other = swap(later, "cls", 1)
     sums = jnp.zeros((2, images.shape[0], 2 * classes * orients), jnp.float32)
     sums = score(w2, [near, other], sums, parity)
     gots, sums, far = lax.optimization_barrier((gots, sums, far))

time: 67.9 us -> 70.7 us (1.041)
  waiting for transfers between devices: 15.3 us -> 18.5 us
    ppermute x14, waiting for transfers between devices: 15.3 us -> 18.5 us  [swap(): return lax.ppermute(value, axis, [(i, i ^ mask) for i in range(size)])]
  transfers between devices with their start and end apart: 14 -> 14, of which waited for: 5 -> 6; matrix products, arithmetic and copies ran while one was open for 1% -> 1% of each run, Pallas kernels for 39% -> 37%
where the time goes in v5:
time: 70.7 us; the launch traced here: 70.4 us
  Pallas kernels  28.9 us (41%)
  starting transfers between devices  19.4 us (27%)
  waiting for transfers between devices  18.5 us (26%)
  local copies, waits for them, and re-layouts  2.59 us (4%)
  between operations  0.81 us (1%)
    ppermute x14, starting transfers between devices, swap(): return lax.ppermute(value, axis, [(i, i ^ mask) for i in range(size)])  19.4 us
    pallas_call x1, Pallas kernels, front(): pl.pallas_call(functools.partial(front_kernel, blocks), grid_spec=pltpu.P...  19.2 us
    ppermute x14, waiting for transfers between devices, swap(): return lax.ppermute(value, axis, [(i, i ^ mask) for i in range(size)])  18.5 us
    pallas_call x2, Pallas kernels, score(): pl.pallas_call(functools.partial(score_kernel, orients, last), grid_spec=...  6.89 us
    pallas_call x1, Pallas kernels, final_sum(): pl.pallas_call(final_kernel, in_specs=[vmem] * (5 + len(gots)), out_specs...  2.35 us
  transfers between devices with their start and end apart: 14, of which 6 were waited for; matrix products, arithmetic and copies ran while one was open for 1% of the time, Pallas kernels for 37%

profile of v5, /device:TPU:0, one launch (start us, length us, event | category | flops | bytes accessed | tf_op | source)
XLA Modules:
  0.0 70.4 jit_solution(2670088866744455110)
XLA Ops:
  0.6 1.1 %dynamic-slice_bitcast_fusion = (bf16[1,64,8,256]{3,1,2,0:T(8,128)(2,1)S(1)}, bf16[1,64,8,256]{3,1,2,0:T(8,128)(2,1)S(1)}) fusion(bf16[1,8,128,256]{3,2,1,0:T(8,128)(2,1)} %param.12, s32[]{:T(128)S(6)} %select_n.10, s32[]{:T(128)S(6)} %select_n.4), kind=kLoop, calls=%fused_computation.4 | loop fusion | bytes 1048584 | tf_op jit(solution)/shard_map/transpose | solution.py:375
  1.7 0.2 copy.17
  1.9 3.1 %collective-permute-start = (bf16[1,512,256]{2,1,0:T(8,128)(2,1)S(1)}, bf16[1,512,256]{2,1,0:T(8,128)(2,1)S(1)}, u32[]{:S(2)}, u32[]{:S(2)}) collective-permute-start(bf16[1,512,256]{2,1,0:T(8,128)(2,1)S(1)} %bitcast.16), channel_id=1, source_target_pairs={{0,2},{1,3},{2,0},{3,1},{4,6},{5,7},{6,4},{7,5},{8,10},{9,11},{10,... | collective-permute-start | bytes 786440 | tf_op jit(solution)/shard_map/ppermute | solution.py:358
  5.0 2.6 %collective-permute-start.1 = (bf16[1,512,256]{2,1,0:T(8,128)(2,1)S(1)}, bf16[1,512,256]{2,1,0:T(8,128)(2,1)S(1)}, u32[]{:S(2)}, u32[]{:S(2)}) collective-permute-start(bf16[1,512,256]{2,1,0:T(8,128)(2,1)S(1)} %bitcast.17), channel_id=1, source_target_pairs={{0,4},{1,5},{2,6},{3,7},{4,0},{5,1},{6,2},{7,3},{8,12},{9,13},{10,... | collective-permute-start | bytes 786440 | tf_op jit(solution)/shard_map/ppermute | solution.py:358
  7.6 19.2 %front.1 = (bf16[128,96,256]{2,1,0:T(8,128)(2,1)}, f32[4,512,256]{2,1,0:T(8,128)S(1)}, bf16[4,520,256]{2,1,0:T(8,128)(2,1)S(1)}, f32[4,8,128]{2,1,0:T(8,128)S(1)}) custom-call(s32[96]{0:T(128)} %bitcast.24, s32[96]{0:T(128)} %orient_ref.1, s32[96]{0:T(128)} %bin_ref.1, bf16[96,256,256]{2,1,0:T(8,128)(2,1)} %img_ref.1, ...), custom_call_target="tpu_custom_call" | custom-call | flops 12884901888 | bytes 25165824 | tf_op jit(solution)/shard_map/front/pallas_call | solution.py:108
  26.8 0.1 collective-permute-start.3
  26.9 0.1 pad_maximum_fusion.refs_0_
  27.0 2.5 %collective-permute-done.3.got_ref = bf16[4,520,256]{2,1,0:T(8,128)(2,1)S(1)} collective-permute-done((bf16[4,520,256]{2,1,0:T(8,128)(2,1)S(1)}, bf16[4,520,256]{2,1,0:T(8,128)(2,1)S(1)}, u32[]{:S(2)}, u32[]{:S(2)}) %collective-permute-start.3) | collective-permute-done | bytes 1064992 | tf_op jit(solution)/shard_map/ppermute | solution.py:358
  29.5 0.3 chip_sum.1
  29.8 0.2 collective-permute-start.7
  30.1 0.1 fusion
  30.2 1.8 %collective-permute-start.8 = (bf16[3,256,256]{2,1,0:T(8,128)(2,1)S(1)}, bf16[3,256,256]{2,1,0:T(8,128)(2,1)S(1)}, u32[]{:S(2)}, u32[]{:S(2)}) collective-permute-start(bf16[3,256,256]{2,1,0:T(8,128)(2,1)S(1)} %get-tuple-element.66), channel_id=1, source_target_pairs={{0,8},{8,0},{16,24},{24,16},{1,9},{9,1},{17,25},{25,17},{2,10},{10... | collective-permute-start | bytes 1179656 | tf_op jit(solution)/shard_map/ppermute | solution.py:358
  32.0 1.5 %collective-permute-start.9 = (bf16[3,256,256]{2,1,0:T(8,128)(2,1)S(1)}, bf16[3,256,256]{2,1,0:T(8,128)(2,1)S(1)}, u32[]{:S(2)}, u32[]{:S(2)}) collective-permute-start(bf16[3,256,256]{2,1,0:T(8,128)(2,1)S(1)} %get-tuple-element.65), channel_id=1, source_target_pairs={{0,16},{8,24},{16,0},{24,8},{1,17},{9,25},{17,1},{25,9},{2,18},{10... | collective-permute-start | bytes 1179656 | tf_op jit(solution)/shard_map/ppermute | solution.py:358
  33.5 0.5 collective-permute-start.4
  34.0 0.3 collective-permute-start.5
  34.3 2.7 %collective-permute-start.6 = (bf16[4,136,256]{2,1,0:T(8,128)(2,1)S(1)}, bf16[4,136,256]{2,1,0:T(8,128)(2,1)S(1)}, u32[]{:S(2)}, u32[]{:S(2)}) collective-permute-start(bf16[4,136,256]{2,1,0:T(8,128)(2,1)S(1)} %get-tuple-element.42), channel_id=1, source_target_pairs={{0,24},{8,16},{16,8},{24,0},{1,25},{9,17},{17,9},{25,1},{2,26},{10... | collective-permute-start | bytes 835592 | tf_op jit(solution)/shard_map/ppermute | solution.py:358
  37.0 0.1 copy.16
  37.2 3.1 %score.2.sum_ref = f32[2,96,128]{2,1,0:T(8,128)S(1)} custom-call(s32[1]{0:T(128)} %bitcast.3.first_ref, f32[2,96,128]{2,1,0:T(8,128)S(1)} %broadcast_in_dim.16.sum_ref, bf16[128,96,256]{2,1,0:T(8,128)(2,1)} %get-tuple-element.43.w_ref, bf16[4,512,256]{2,1,0:T(8,128)(2,1)} %copy-done.3, bf16[4,512,256]{2,1,0:T(8,128)(2,1)} %copy-done.5), custom_call_target="tpu_custom_call" | custom-call | tf_op jit(solution)/shard_map/score/pallas_call | solution.py:203
  40.3 1.9 %collective-permute-done.8 = bf16[3,256,256]{2,1,0:T(8,128)(2,1)S(1)} collective-permute-done((bf16[3,256,256]{2,1,0:T(8,128)(2,1)S(1)}, bf16[3,256,256]{2,1,0:T(8,128)(2,1)S(1)}, u32[]{:S(2)}, u32[]{:S(2)}) %collective-permute-start.8) | collective-permute-done | bytes 393248 | tf_op jit(solution)/shard_map/ppermute | solution.py:358
  42.2 1.7 %collective-permute-done.9 = bf16[3,256,256]{2,1,0:T(8,128)(2,1)S(1)} collective-permute-done((bf16[3,256,256]{2,1,0:T(8,128)(2,1)S(1)}, bf16[3,256,256]{2,1,0:T(8,128)(2,1)S(1)}, u32[]{:S(2)}, u32[]{:S(2)}) %collective-permute-start.9) | collective-permute-done | bytes 393248 | tf_op jit(solution)/shard_map/ppermute | solution.py:358
  43.9 4.2 %collective-permute-done.4.refs_0_ = bf16[4,136,256]{2,1,0:T(8,128)(2,1)S(1)} collective-permute-done((bf16[4,136,256]{2,1,0:T(8,128)(2,1)S(1)}, bf16[4,136,256]{2,1,0:T(8,128)(2,1)S(1)}, u32[]{:S(2)}, u32[]{:S(2)}) %collective-permute-start.4) | collective-permute-done | bytes 278560 | tf_op jit(solution)/shard_map/ppermute | solution.py:358
  48.2 6.8 %collective-permute-done.5.refs_1_ = bf16[4,136,256]{2,1,0:T(8,128)(2,1)S(1)} collective-permute-done((bf16[4,136,256]{2,1,0:T(8,128)(2,1)S(1)}, bf16[4,136,256]{2,1,0:T(8,128)(2,1)S(1)}, u32[]{:S(2)}, u32[]{:S(2)}) %collective-permute-start.5) | collective-permute-done | bytes 278560 | tf_op jit(solution)/shard_map/ppermute | solution.py:358
  55.0 0.1 maximum_maximum_fusion.refs_0_
  55.1 0.1 collective-permute-start.13
  55.2 0.2 plane_sum.1
  55.3 4.1 %collective-permute-start.10 = (bf16[136,256]{1,0:T(8,128)(2,1)S(1)}, bf16[136,256]{1,0:T(8,128)(2,1)S(1)}, u32[]{:S(2)}, u32[]{:S(2)}) collective-permute-start(bf16[136,256]{1,0:T(8,128)(2,1)S(1)} %get-tuple-element.51), channel_id=1, source_target_pairs={{0,2},{1,3},{2,0},{3,1},{4,6},{5,7},{6,4},{7,5},{8,10},{9,11},{10,... | collective-permute-start | bytes 208904 | tf_op jit(solution)/shard_map/ppermute | solution.py:358
  59.4 1.1 %collective-permute-start.11 = (bf16[136,256]{1,0:T(8,128)(2,1)S(1)}, bf16[136,256]{1,0:T(8,128)(2,1)S(1)}, u32[]{:S(2)}, u32[]{:S(2)}) collective-permute-start(bf16[136,256]{1,0:T(8,128)(2,1)S(1)} %get-tuple-element.52), channel_id=1, source_target_pairs={{0,4},{1,5},{2,6},{3,7},{4,0},{5,1},{6,2},{7,3},{8,12},{9,13},{10,... | collective-permute-start | bytes 208904 | tf_op jit(solution)/shard_map/ppermute | solution.py:358
  60.5 1.4 %collective-permute-start.12 = (bf16[136,256]{1,0:T(8,128)(2,1)S(1)}, bf16[136,256]{1,0:T(8,128)(2,1)S(1)}, u32[]{:S(2)}, u32[]{:S(2)}) collective-permute-start(bf16[136,256]{1,0:T(8,128)(2,1)S(1)} %get-tuple-element.53), channel_id=1, source_target_pairs={{0,6},{1,7},{2,4},{3,5},{4,2},{5,3},{6,0},{7,1},{8,14},{9,15},{10,... | collective-permute-start | bytes 208904 | tf_op jit(solution)/shard_map/ppermute | solution.py:358
  61.9 1.1 %copy-done.6 = bf16[4,512,256]{2,1,0:T(8,128)(2,1)} copy-done((bf16[4,512,256]{2,1,0:T(8,128)(2,1)}, bf16[4,512,256]{2,1,0:T(8,128)(2,1)S(1)}, u32[]{:S(2)}) %copy-start.6) | copy-done | bytes 1048600
  63.0 3.8 %score.3 = f32[1,96]{1,0:T(1,128)} custom-call(s32[1]{0:T(128)} %bitcast.4.first_ref, f32[2,96,128]{2,1,0:T(8,128)S(1)} %score.2.sum_ref, bf16[128,96,256]{2,1,0:T(8,128)(2,1)} %get-tuple-element.43.w_ref, bf16[4,512,256]{2,1,0:T(8,128)(2,1)} %copy-done.4, bf16[4,512,256]{2,1,0:T(8,128)(2,1)} %copy-done.6), custom_call_target="tpu_custom_call" | custom-call | tf_op jit(solution)/shard_map/score/pallas_call | solution.py:203
  66.8 1.2 %collective-permute-done.11.refs_1_ = bf16[136,256]{1,0:T(8,128)(2,1)S(1)} collective-permute-done((bf16[136,256]{1,0:T(8,128)(2,1)S(1)}, bf16[136,256]{1,0:T(8,128)(2,1)S(1)}, u32[]{:S(2)}, u32[]{:S(2)}) %collective-permute-start.11) | collective-permute-done | bytes 69664 | tf_op jit(solution)/shard_map/ppermute | solution.py:358
  68.1 2.4 %final_sum.1 = (f32[128,256]{1,0:T(8,128)}, f32[128,256]{1,0:T(8,128)}) custom-call(f32[16,128,256]{2,1,0:T(8,128)S(1)} %copy-done, s32[8,128]{1,0:T(8,128)S(1)} %copy-done.1, f32[8,128]{1,0:T(8,128)S(1)} %copy-done.2, f32[128,256]{1,0:T(8,128)S(1)} %get-tuple-element.58.own_ref, f32[8,128]{1,0:T(8,128)S(1)} %get-tuple-element.59.count_ref, ...), custom_call_target="tpu_custom_call" | custom-call | tf_op jit(solution)/shard_map/final_sum/pallas_call | solution.py:342
  (26 shorter events, 0.1 us)
Async XLA Ops:
  1.9 24.9 %collective-permute-start = (bf16[1,512,256]{2,1,0:T(8,128)(2,1)S(1)}, bf16[1,512,256]{2,1,0:T(8,128)(2,1)S(1)}, u32[]{:S(2)}, u32[]{:S(2)}) collective-permute-start(bf16[1,512,256]{2,1,0:T(8,128)(2,1)S(1)} %bitcast.16), channel_id=1, source_target_pairs={{0,2},{1,3},{2,0},{3,1},{4,6},{5,7},{6,4},{7,5},{8,10},{9,11},{10,... | collective-permute-start | bytes 786440 | tf_op jit(solution)/shard_map/ppermute | solution.py:358
  5.0 21.8 %collective-permute-start.1 = (bf16[1,512,256]{2,1,0:T(8,128)(2,1)S(1)}, bf16[1,512,256]{2,1,0:T(8,128)(2,1)S(1)}, u32[]{:S(2)}, u32[]{:S(2)}) collective-permute-start(bf16[1,512,256]{2,1,0:T(8,128)(2,1)S(1)} %bitcast.17), channel_id=1, source_target_pairs={{0,4},{1,5},{2,6},{3,7},{4,0},{5,1},{6,2},{7,3},{8,12},{9,13},{10,... | collective-permute-start | bytes 786440 | tf_op jit(solution)/shard_map/ppermute | solution.py:358
  7.6 19.2 %collective-permute-start.2 = (bf16[1,512,256]{2,1,0:T(8,128)(2,1)S(1)}, bf16[1,512,256]{2,1,0:T(8,128)(2,1)S(1)}, u32[]{:S(2)}, u32[]{:S(2)}) collective-permute-start(bf16[1,512,256]{2,1,0:T(8,128)(2,1)S(1)} %bitcast.18), channel_id=1, source_target_pairs={{0,6},{1,7},{2,4},{3,5},{4,2},{5,3},{6,0},{7,1},{8,14},{9,15},{10,... | collective-permute-start | bytes 786440 | tf_op jit(solution)/shard_map/ppermute | solution.py:358
  26.8 2.7 %collective-permute-start.3 = (bf16[4,520,256]{2,1,0:T(8,128)(2,1)S(1)}, bf16[4,520,256]{2,1,0:T(8,128)(2,1)S(1)}, u32[]{:S(2)}, u32[]{:S(2)}) collective-permute-start(bf16[4,520,256]{2,1,0:T(8,128)(2,1)S(1)} %get-tuple-element.37), channel_id=1, source_target_pairs={{0,1},{1,0},{2,3},{3,2},{4,5},{5,4},{6,7},{7,6},{8,9},{9,8},{10,11... | collective-permute-start | bytes 3194888 | tf_op jit(solution)/shard_map/ppermute | solution.py:358
  27.0 3.1 %copy-start.3 = (bf16[4,512,256]{2,1,0:T(8,128)(2,1)}, bf16[4,512,256]{2,1,0:T(8,128)(2,1)S(1)}, u32[]{:S(2)}) copy-start(bf16[4,512,256]{2,1,0:T(8,128)(2,1)S(1)} %pad_maximum_fusion.refs_0_) | copy-start | bytes 3145732
  29.8 4.5 %collective-permute-start.7 = (bf16[4,512,256]{2,1,0:T(8,128)(2,1)S(1)}, bf16[4,512,256]{2,1,0:T(8,128)(2,1)S(1)}, u32[]{:S(2)}, u32[]{:S(2)}) collective-permute-start(bf16[4,512,256]{2,1,0:T(8,128)(2,1)S(1)} %pad_maximum_fusion.refs_0_), channel_id=1, source_target_pairs={{0,1},{1,0},{2,3},{3,2},{4,5},{5,4},{6,7},{7,6},{8,9},{9,8},{10,11... | collective-permute-start | bytes 3145736 | tf_op jit(solution)/shard_map/ppermute | solution.py:358
  30.2 12.0 %collective-permute-start.8 = (bf16[3,256,256]{2,1,0:T(8,128)(2,1)S(1)}, bf16[3,256,256]{2,1,0:T(8,128)(2,1)S(1)}, u32[]{:S(2)}, u32[]{:S(2)}) collective-permute-start(bf16[3,256,256]{2,1,0:T(8,128)(2,1)S(1)} %get-tuple-element.66), channel_id=1, source_target_pairs={{0,8},{8,0},{16,24},{24,16},{1,9},{9,1},{17,25},{25,17},{2,10},{10... | collective-permute-start | bytes 1179656 | tf_op jit(solution)/shard_map/ppermute | solution.py:358
  32.0 12.0 %collective-permute-start.9 = (bf16[3,256,256]{2,1,0:T(8,128)(2,1)S(1)}, bf16[3,256,256]{2,1,0:T(8,128)(2,1)S(1)}, u32[]{:S(2)}, u32[]{:S(2)}) collective-permute-start(bf16[3,256,256]{2,1,0:T(8,128)(2,1)S(1)} %get-tuple-element.65), channel_id=1, source_target_pairs={{0,16},{8,24},{16,0},{24,8},{1,17},{9,25},{17,1},{25,9},{2,18},{10... | collective-permute-start | bytes 1179656 | tf_op jit(solution)/shard_map/ppermute | solution.py:358
  33.5 14.7 %collective-permute-start.4 = (bf16[4,136,256]{2,1,0:T(8,128)(2,1)S(1)}, bf16[4,136,256]{2,1,0:T(8,128)(2,1)S(1)}, u32[]{:S(2)}, u32[]{:S(2)}) collective-permute-start(bf16[4,136,256]{2,1,0:T(8,128)(2,1)S(1)} %get-tuple-element.40), channel_id=1, source_target_pairs={{0,8},{8,0},{16,24},{24,16},{1,9},{9,1},{17,25},{25,17},{2,10},{10... | collective-permute-start | bytes 835592 | tf_op jit(solution)/shard_map/ppermute | solution.py:358
  34.0 21.0 %collective-permute-start.5 = (bf16[4,136,256]{2,1,0:T(8,128)(2,1)S(1)}, bf16[4,136,256]{2,1,0:T(8,128)(2,1)S(1)}, u32[]{:S(2)}, u32[]{:S(2)}) collective-permute-start(bf16[4,136,256]{2,1,0:T(8,128)(2,1)S(1)} %get-tuple-element.41), channel_id=1, source_target_pairs={{0,16},{8,24},{16,0},{24,8},{1,17},{9,25},{17,1},{25,9},{2,18},{10... | collective-permute-start | bytes 835592 | tf_op jit(solution)/shard_map/ppermute | solution.py:358
  34.3 2.8 %copy-start.5 = (bf16[4,512,256]{2,1,0:T(8,128)(2,1)}, bf16[4,512,256]{2,1,0:T(8,128)(2,1)S(1)}, u32[]{:S(2)}) copy-start(bf16[4,512,256]{2,1,0:T(8,128)(2,1)S(1)} %collective-permute-done.7.refs_1_) | copy-start | bytes 3145732
  34.3 20.7 %collective-permute-start.6 = (bf16[4,136,256]{2,1,0:T(8,128)(2,1)S(1)}, bf16[4,136,256]{2,1,0:T(8,128)(2,1)S(1)}, u32[]{:S(2)}, u32[]{:S(2)}) collective-permute-start(bf16[4,136,256]{2,1,0:T(8,128)(2,1)S(1)} %get-tuple-element.42), channel_id=1, source_target_pairs={{0,24},{8,16},{16,8},{24,0},{1,25},{9,17},{17,9},{25,1},{2,26},{10... | collective-permute-start | bytes 835592 | tf_op jit(solution)/shard_map/ppermute | solution.py:358
  55.1 6.8 %copy-start.4 = (bf16[4,512,256]{2,1,0:T(8,128)(2,1)}, bf16[4,512,256]{2,1,0:T(8,128)(2,1)S(1)}, u32[]{:S(2)}) copy-start(bf16[4,512,256]{2,1,0:T(8,128)(2,1)S(1)} %maximum_maximum_fusion.refs_0_) | copy-start | bytes 3145732
  55.1 6.8 %collective-permute-start.13 = (bf16[4,512,256]{2,1,0:T(8,128)(2,1)S(1)}, bf16[4,512,256]{2,1,0:T(8,128)(2,1)S(1)}, u32[]{:S(2)}, u32[]{:S(2)}) collective-permute-start(bf16[4,512,256]{2,1,0:T(8,128)(2,1)S(1)} %maximum_maximum_fusion.refs_0_), channel_id=1, source_target_pairs={{0,1},{1,0},{2,3},{3,2},{4,5},{5,4},{6,7},{7,6},{8,9},{9,8},{10,11... | collective-permute-start | bytes 3145736 | tf_op jit(solution)/shard_map/ppermute | solution.py:358
  55.3 11.5 %collective-permute-start.10 = (bf16[136,256]{1,0:T(8,128)(2,1)S(1)}, bf16[136,256]{1,0:T(8,128)(2,1)S(1)}, u32[]{:S(2)}, u32[]{:S(2)}) collective-permute-start(bf16[136,256]{1,0:T(8,128)(2,1)S(1)} %get-tuple-element.51), channel_id=1, source_target_pairs={{0,2},{1,3},{2,0},{3,1},{4,6},{5,7},{6,4},{7,5},{8,10},{9,11},{10,... | collective-permute-start | bytes 208904 | tf_op jit(solution)/shard_map/ppermute | solution.py:358
  59.4 8.6 %collective-permute-start.11 = (bf16[136,256]{1,0:T(8,128)(2,1)S(1)}, bf16[136,256]{1,0:T(8,128)(2,1)S(1)}, u32[]{:S(2)}, u32[]{:S(2)}) collective-permute-start(bf16[136,256]{1,0:T(8,128)(2,1)S(1)} %get-tuple-element.52), channel_id=1, source_target_pairs={{0,4},{1,5},{2,6},{3,7},{4,0},{5,1},{6,2},{7,3},{8,12},{9,13},{10,... | collective-permute-start | bytes 208904 | tf_op jit(solution)/shard_map/ppermute | solution.py:358
  60.5 7.5 %collective-permute-start.12 = (bf16[136,256]{1,0:T(8,128)(2,1)S(1)}, bf16[136,256]{1,0:T(8,128)(2,1)S(1)}, u32[]{:S(2)}, u32[]{:S(2)}) collective-permute-start(bf16[136,256]{1,0:T(8,128)(2,1)S(1)} %get-tuple-element.53), channel_id=1, source_target_pairs={{0,6},{1,7},{2,4},{3,5},{4,2},{5,3},{6,0},{7,1},{8,14},{9,15},{10,... | collective-permute-start | bytes 208904 | tf_op jit(solution)/shard_map/ppermute | solution.py:358
  61.9 1.1 %copy-start.6 = (bf16[4,512,256]{2,1,0:T(8,128)(2,1)}, bf16[4,512,256]{2,1,0:T(8,128)(2,1)S(1)}, u32[]{:S(2)}) copy-start(bf16[4,512,256]{2,1,0:T(8,128)(2,1)S(1)} %collective-permute-done.13.refs_1_) | copy-start | bytes 3145732
  63.0 5.1 %copy-start = (f32[16,128,256]{2,1,0:T(8,128)S(1)}, f32[16,128,256]{2,1,0:T(8,128)}, u32[]{:S(2)}) copy-start(f32[16,128,256]{2,1,0:T(8,128)} %ctf_ref.3) | copy-start | bytes 6291460
  63.0 5.1 %copy-start.1 = (s32[8,128]{1,0:T(8,128)S(1)}, s32[8,128]{1,0:T(8,128)}, u32[]{:S(2)}) copy-start(s32[8,128]{1,0:T(8,128)} %slot_ref.3) | copy-start | bytes 12292
  63.0 5.1 %copy-start.2 = (f32[8,128]{1,0:T(8,128)S(1)}, f32[8,128]{1,0:T(8,128)}, u32[]{:S(2)}) copy-start(f32[8,128]{1,0:T(8,128)} %wt_ref.3) | copy-start | bytes 12292
